TPU v7x, 512 devices: a whole 4x8x8 slice. The times are simulated.
512 devices in a mesh: row: 32 (over y, x), col: 16 (over z, core).
Axes of the slice: x: 4, y: 8, z: 8, core: 2. Of those that a mesh axis runs over, the one named last changes fastest.
Arguments:
- kernel_matrix: float32 [16384, 16384], P('row', 'col'), may hold values from 0 to 2, as said below
Outputs:
- factored: float32 [16384, 16384], P('row', 'col')
Inputs may be any that keep to these rules, and one draw needn't show every extreme that they name: kernel_matrix, put in global order by the element-cyclic map, is symmetric: a Gaussian-process kernel amp * exp(-distance / scale) over random points plus a nugget of at least 0.5 on the diagonal, so it is positive definite with smallest eigenvalue at least 0.5.
All inputs are finite; a program needn't handle non-finite values.
Results may differ from a plain program's by a relative error of at most 0.00025.
Values sent between devices are 32-bit elements; how exact they have to be, the bound alone decides.
No kernel may reach another device: no remote copies, remote signals or barrier semaphores. Data moves between devices by JAX's collectives and lax.ppermute only.
A program may use at most 64 MiB of HBM per device.

v0:
```python
import jax
import jax.numpy as jnp
from jax import lax
from jax.sharding import PartitionSpec as P

PANEL = 192
PANELS = 2


def spread(block, axis, source):
    block = jnp.where(lax.axis_index(axis) == source, block, jnp.zeros_like(block))
    return lax.psum(block, axis)


def solve_rows(lower_factor, rows):
    return lax.linalg.triangular_solve(
        lower_factor, rows, left_side=False, lower=True, transpose_a=True
    )


def alternate_cols(block, groups):
    height = block.shape[0]
    inner = block.shape[1] // groups
    return block.reshape(height, groups, inner).transpose(0, 2, 1).reshape(height, groups * inner)


def alternate_rows(block, groups):
    inner = block.shape[0] // groups
    breadth = block.shape[1]
    return block.reshape(groups, inner, breadth).transpose(1, 0, 2).reshape(groups * inner, breadth)


def per_device(kernel_matrix):
    matrix = kernel_matrix
    row_count = lax.axis_size("row")
    col_count = lax.axis_size("col")
    row_share = row_count // col_count
    local_rows, local_cols = matrix.shape
    tile_rows = PANEL // row_count
    tile_cols = PANEL // col_count
    col_index = lax.axis_index("col")
    for current in range(PANELS):
        factor_row_start = current * tile_rows
        factor_col_start = current * tile_cols
        factor_col_rest = factor_col_start + tile_cols
        corner = matrix[
            factor_row_start : factor_row_start + tile_rows, factor_col_start:factor_col_rest
        ]
        corner = lax.all_gather(corner, "row", axis=0, tiled=True)
        corner = lax.all_gather(corner, "col", axis=1, tiled=True)
        corner = alternate_cols(alternate_rows(corner, row_count), col_count)
        lower_factor = jnp.linalg.cholesky(corner)
        column_block = matrix[:, factor_col_start:factor_col_rest]
        gathered = alternate_cols(
            lax.all_gather(column_block, "col", axis=1, tiled=True), col_count
        )
        factor_left_rows = solve_rows(lower_factor, gathered)
        received = []
        for source in range(row_share):
            received.append(spread(factor_left_rows, "row", col_index + source * col_count))
        factor_right_rows = jnp.stack(received, axis=1).reshape(local_cols, PANEL)[factor_col_rest:]
        row_start = current * tile_rows
        col_start = current * tile_cols
        owned = factor_left_rows.reshape(local_rows, tile_cols, col_count)
        owned = lax.dynamic_index_in_dim(owned, col_index, axis=2, keepdims=False)
        matrix = matrix.at[row_start:, col_start : col_start + tile_cols].set(owned[row_start:])
        row_low = (current + 1) * tile_rows
        col_low = (current + 1) * tile_cols
        term = jnp.dot(
            factor_left_rows[row_low:local_rows],
            factor_right_rows.T,
            precision=lax.Precision.HIGHEST,
            preferred_element_type=jnp.float32,
        )
        matrix = matrix.at[row_low:local_rows, col_low:local_cols].add(-term)
    return matrix


def solution(mesh):
    in_specs = (P("row", "col"),)
    out_specs = P("row", "col")
    return jax.shard_map(
        per_device, mesh=mesh, in_specs=in_specs, out_specs=out_specs, check_vma=False
    )
```

profile of v0, /device:TPU:1, one launch (start us, length us, event | category | flops | bytes accessed | tf_op | source)
XLA Modules:
  0.0 627.2 jit_solution(13229825803608452660)
XLA Ops:
  6.5 1.9 copy.35
  8.5 0.7 slice_bitcast_fusion.12
  9.2 25.9 %all-gather.2 = f32[16,12,512]{2,1,0:T(8,128)S(1)} all-gather(f32[1,12,512]{2,1,0:T(8,128)S(1)} %slice_bitcast_fusion.11), channel_id=1, replica_groups=mesh['row'=32,'col'=16] {'col'}, dimensions={0}, use_global_device_ids=true | all-gather | bytes 417792 | tf_op jit(solution)/shard_map/all_gather | solution.py:55
  35.4 31.9 %all-gather = f32[32,6,12]{2,1,0:T(8,128)S(1)} all-gather(f32[1,6,12]{2,1,0:T(8,128)S(1)} %slice_bitcast_fusion.12), channel_id=1, replica_groups=mesh['row'=32,'col'=16] {'row'}, dimensions={0}, use_global_device_ids=true | all-gather | bytes 9504 | tf_op jit(solution)/shard_map/all_gather | solution.py:49
  67.4 23.0 %all-gather.1 = f32[16,12,192]{2,1,0:T(8,128)S(1)} all-gather(f32[1,12,192]{2,1,0:T(8,128)S(1)} %bitcast.133), channel_id=1, replica_groups=mesh['row'=32,'col'=16] {'col'}, dimensions={0}, use_global_device_ids=true | all-gather | bytes 156672 | tf_op jit(solution)/shard_map/all_gather | solution.py:50
  90.5 0.3 copy.30
  91.4 11.7 %cholesky.136 = f32[128,128]{1,0:T(8,128)S(1)} custom-call(f32[128,128]{1,0:T(8,128)S(1)} %cholesky.208), custom_call_target="Cholesky" | custom-call | tf_op jit(solution)/shard_map/jit(cholesky)/cholesky | solution.py:52
  103.2 9.8 %custom-call.13 = f32[1,128,128]{1,2,0:T(8,128)S(1)} custom-call(f32[1,128,128]{2,1,0:T(8,128)S(1)} %get-tuple-element.94), custom_call_target="InvertDiagBlocksLowerTriangular" | custom-call | tf_op jit(solution)/shard_map/jit(cholesky)/cholesky | solution.py:52
  113.4 5.8 cholesky.156
  119.2 0.6 compare_reduce_fusion.3
  119.9 0.7 compare_reduce_fusion.2
  122.0 0.6 copy-done.1
  122.7 19.7 %custom-call.14 = f32[2,128,128]{1,2,0:T(8,128)S(1)} custom-call(f32[2,128,128]{2,1,0:T(8,128)S(1)} %pad_maximum_fusion.4), custom_call_target="InvertDiagBlocksLowerTriangular" | custom-call | tf_op jit(solution)/shard_map/triangular_solve/custom-call.0 | solution.py:16
  142.4 0.6 copy-done.3
  143.1 0.4 fusion.6
  143.8 1.1 fusion.19
  144.9 1.0 select_bitcast_fusion.3
  146.2 0.6 compare_reduce_fusion.4
  146.8 0.6 bitcast_select_fusion
  147.4 0.3 scatter.6
  147.7 148.2 %all-reduce.10.cloned.1.call-done = (f32[512,1,192]{0,2,1:T(8,128)}, f32[512,1,192]{0,2,1:T(8,128)}) async-done(((f32[512,1,192]{0,2,1:T(8,128)}, f32[512,1,192]{0,2,1:T(8,128)}), (f32[512,1,192]{0,2,1:T(8,128)}, f32[512,1,192]{0,2,1:T(8,128)})) %all-reduce.10.cloned.1.call-update) | async-done | bytes 786448 | tf_op jit(solution)/shard_map/psum | solution.py:12
  295.9 1.4 pad_maximum_fusion.1
  297.3 1.3 copy.36
  298.6 1.9 slice.169
  300.5 2.1 slice_add_fusion
  302.6 1.3 copy-done
  304.0 28.6 %all-gather.3 = f32[32,6,12]{2,1,0:T(8,128)S(1)} all-gather(f32[1,6,12]{2,1,0:T(8,128)S(1)} %bitcast.135), channel_id=1, replica_groups=mesh['row'=32,'col'=16] {'row'}, dimensions={0}, use_global_device_ids=true | all-gather | bytes 9504 | tf_op jit(solution)/shard_map/all_gather | solution.py:49
  332.8 32.5 %all-gather.4 = f32[16,12,192]{2,1,0:T(8,128)S(1)} all-gather(f32[1,12,192]{2,1,0:T(8,128)S(1)} %bitcast.134), channel_id=1, replica_groups=mesh['row'=32,'col'=16] {'col'}, dimensions={0}, use_global_device_ids=true | all-gather | bytes 156672 | tf_op jit(solution)/shard_map/all_gather | solution.py:50
  365.4 0.3 copy.40
  366.3 11.7 %cholesky.174 = f32[128,128]{1,0:T(8,128)S(1)} custom-call(f32[128,128]{1,0:T(8,128)S(1)} %cholesky.211), custom_call_target="Cholesky" | custom-call | tf_op jit(solution)/shard_map/jit(cholesky)/cholesky | solution.py:52
  378.0 9.8 %custom-call.15 = f32[1,128,128]{1,2,0:T(8,128)S(1)} custom-call(f32[1,128,128]{2,1,0:T(8,128)S(1)} %get-tuple-element.92), custom_call_target="InvertDiagBlocksLowerTriangular" | custom-call | tf_op jit(solution)/shard_map/jit(cholesky)/cholesky | solution.py:52
  388.2 5.8 cholesky.194
  394.1 0.7 compare_reduce_fusion.1
  394.8 0.6 compare_reduce_fusion
  396.8 10.9 %scatter-add.6 = f32[512,1024]{0,1:T(8,128)S(1)} dynamic-update-slice(f32[512,1024]{0,1:T(8,128)S(1)} %scatter.6, f32[506,1012]{0,1:T(8,128)} %copy-done, s32[]{:T(128)} %constant.182.clone.1, s32[]{:T(128)} %constant.183.clone.1) | dynamic-update-slice | bytes 4096580 | tf_op jit(solution)/shard_map/scatter-add | solution.py:75
  407.7 16.4 %all-gather.5 = f32[16,12,512]{2,1,0:T(8,128)S(1)} all-gather(f32[1,12,512]{2,1,0:T(8,128)S(1)} %slice_bitcast_fusion.8), channel_id=1, replica_groups=mesh['row'=32,'col'=16] {'col'}, dimensions={0}, use_global_device_ids=true | all-gather | bytes 417792 | tf_op jit(solution)/shard_map/all_gather | solution.py:55
  424.5 19.7 %custom-call.16 = f32[2,128,128]{1,2,0:T(8,128)S(1)} custom-call(f32[2,128,128]{2,1,0:T(8,128)S(1)} %pad_maximum_fusion.5), custom_call_target="InvertDiagBlocksLowerTriangular" | custom-call | tf_op jit(solution)/shard_map/triangular_solve/custom-call.0 | solution.py:16
  444.2 0.4 fusion.4
  444.9 0.3 fusion.16
  445.2 1.0 select_bitcast_fusion.1
  446.4 1.1 scatter.9
  447.5 149.9 %all-reduce.8.cloned.1.call-done = (f32[512,1,192]{0,2,1:T(8,128)}, f32[512,1,192]{0,2,1:T(8,128)}) async-done(((f32[512,1,192]{0,2,1:T(8,128)}, f32[512,1,192]{0,2,1:T(8,128)}), (f32[512,1,192]{0,2,1:T(8,128)}, f32[512,1,192]{0,2,1:T(8,128)})) %all-reduce.8.cloned.1.call-update) | async-done | bytes 786448 | tf_op jit(solution)/shard_map/psum | solution.py:12
  597.4 2.3 pad_maximum_fusion
  599.7 1.9 copy.45
  601.6 1.7 slice.176
  603.3 4.5 slice_add_fusion.1
  607.8 10.8 %scatter-add.9 = f32[512,1024]{0,1:T(8,128)S(1)} dynamic-update-slice(f32[512,1024]{0,1:T(8,128)S(1)} %scatter.9, f32[500,1000]{0,1:T(8,128)} %slice_add_fusion.1, s32[]{:T(128)} %constant.183.clone.1, s32[]{:T(128)} %constant.184.clone.1) | dynamic-update-slice | bytes 4000004 | tf_op jit(solution)/shard_map/scatter-add | solution.py:75
  618.6 1.8 copy.46
  (65 shorter events, 4.4 us)
Async XLA Ops:
  6.5 289.4 %all-reduce.10.cloned.1.call-start = ((), (), s32[]{:S(2)}) async-start(), calls=%async_computation.1 | async-start | bytes 1572864 | tf_op jit(solution)/shard_map/psum | solution.py:12
  122.0 0.6 copy-start.1
  142.4 0.7 copy-start.3
  145.9 451.5 %all-reduce.8.cloned.1.call-start = ((), (), s32[]{:S(2)}) async-start(), calls=%async_computation | async-start | bytes 1572864 | tf_op jit(solution)/shard_map/psum | solution.py:12
  302.6 1.3 copy-start
  407.7 16.7 %copy-start.2 = (f32[128,64]{1,0:T(8,128)S(1)}, f32[128,64]{1,0:T(8,128)}, u32[]{:S(2)}) copy-start(f32[128,64]{1,0:T(8,128)} %copy-done.1) | copy-start | bytes 98308
Sparse Core Ops, SparseCore 0:
  146.1 149.8 all-reduce.9
  446.4 150.9 all-reduce.7
where the time goes:
time: 631 us; the launch traced here: 627 us
  waiting for transfers between devices  298 us (47%)
  blocking collectives  158 us (25%)
  other arithmetic  104 us (16%)
  local copies, waits for them, and re-layouts  39.9 us (6%)
  between operations  16.5 us (3%)
  matrix products  10.1 us (2%)
    psum x2, waiting for transfers between devices, spread(): return lax.psum(block, axis)  298 us
    all_gather x2, blocking collectives, per_device(): corner = lax.all_gather(corner, 'row', axis=0, tiled=True)  60.5 us
    another operation x14, other arithmetic, per_device(): lower_factor = jnp.linalg.cholesky(corner)  57.6 us
    all_gather x2, blocking collectives, per_device(): corner = lax.all_gather(corner, 'col', axis=1, tiled=True)  55.4 us
    all_gather x2, blocking collectives, per_device(): lax.all_gather(column_block, 'col', axis=1, tiled=True)  42.3 us
    another operation x10, other arithmetic, solve_rows(): lax.linalg.triangular_solve(lower_factor, rows, left_side=False, lower=Tr...  39.6 us
    scatter-add x3, local copies, waits for them, and re-layouts, per_device(): matrix = matrix.at[row_low:local_rows, col_low:local_cols].add(-term)  23.4 us
  transfers between devices with their start and end apart: 2, of which 2 were waited for; matrix products, arithmetic and copies ran while one was open for 0% of the time, Pallas kernels for 0%

commit v1 on v0

v1 whole, which is shorter than its diff:
```python
import jax
import jax.numpy as jnp
from jax import lax
from jax.experimental import pallas as pl
from jax.experimental.pallas import tpu as pltpu
from jax.sharding import PartitionSpec as P

PANEL = 192
WIDTH = 384
N_ROW = 32
N_COL = 16
TILE_ROWS = WIDTH // N_ROW
TILE_COLS = WIDTH // N_COL
f32 = jnp.float32


def dot(a, b, over_a, over_b):
    return lax.dot_general(
        a,
        b,
        (((over_a,), (over_b,)), ((), ())),
        precision=lax.Precision.HIGHEST,
        preferred_element_type=f32,
    )


def full(value):
    return jnp.broadcast_to(value, (8, 128))


def factor(block):
    block = list(block)
    count = len(block)
    lane = lax.broadcasted_iota(jnp.int32, (8, 128), 1)
    sub = lax.broadcasted_iota(jnp.int32, (8, 128), 0)
    for q in range(count):
        first = 8 * q
        cols = {
            (i, t): full(block[i][:, first + t : first + t + 1])
            for i in range(q, count)
            for t in range(8)
        }
        e = [[full(cols[q, t][s : s + 1, :]) if s >= t else None for t in range(8)] for s in range(8)]
        scale = [None] * 8
        low = [[None] * 8 for _ in range(8)]
        for t in range(8):
            scale[t] = lax.rsqrt(e[t][t])
            for s in range(t + 1, 8):
                low[s][t] = e[s][t] * scale[t]
            for u in range(t + 1, 8):
                for s in range(u, 8):
                    e[s][u] = e[s][u] - low[s][t] * low[u][t]
        here = (lane >= first) & (lane < first + 8)
        eye = jnp.where(lane - first == sub, 1.0, 0.0).astype(f32)
        own = jnp.where(here, eye, block[q])
        rows = []
        for t in range(8):
            value = full(own[t : t + 1, :])
            for u in range(t):
                value = value - low[t][u] * rows[u]
            rows.append(value * scale[t])
        own = rows[0]
        for t in range(1, 8):
            own = jnp.where(sub == t, rows[t], own)
        block[q] = own
        for i in range(q + 1, count):
            done = []
            total = jnp.where(here, 0.0, block[i])
            for t in range(8):
                value = cols[i, t]
                for u in range(t):
                    value = value - low[t][u] * done[u]
                value = value * scale[t]
                done.append(value)
                total = total - value * rows[t]
            block[i] = total
    return block


def one_hots():
    g = lax.broadcasted_iota(jnp.int32, (WIDTH, WIDTH), 0)
    p = lax.broadcasted_iota(jnp.int32, (WIDTH, WIDTH), 1)
    by_col = jnp.where(p == (g & 15) * TILE_COLS + (g >> 4), 1.0, 0.0).astype(f32)
    by_row = jnp.where(p == (g & 31) * TILE_ROWS + (g >> 5), 1.0, 0.0).astype(f32)
    return by_col, by_row


def factor_kernel(corner_ref, by_row_ref, by_col_ref, s_ref):
    by_col, by_row = one_hots()
    whole = dot(dot(by_col, corner_ref[...], 1, 0), by_row, 1, 1)
    for a in range(3):
        for b in range(3):
            s_ref[a, b] = whole[128 * a : 128 * a + 128, 128 * b : 128 * b + 128]
    row = lax.broadcasted_iota(jnp.int32, (128, 128), 0)
    col = lax.broadcasted_iota(jnp.int32, (128, 128), 1)

    def step(now, _):
        block = factor([s_ref[now, now, 8 * i : 8 * i + 8, :] for i in range(16)])
        inverse = jnp.where(col <= row, jnp.concatenate(block, axis=0), 0.0)
        s_ref[now, now] = inverse
        for b in range(3):

            @pl.when(b != now)
            def _():
                s_ref[now, b] = dot(inverse, s_ref[now, b], 1, 0)

        def update(a, _):
            upper = s_ref[now, a]
            for b in range(3):
                value = dot(upper, s_ref[now, b], 0, 0)

                @pl.when(b != now)
                def _():
                    s_ref[a, b] = s_ref[a, b] - value

                @pl.when(b == now)
                def _():
                    s_ref[a, b] = -value

            return 0

        lax.fori_loop(now + 1, 3, update, 0)
        return 0

    lax.fori_loop(0, 3, step, 0)
    zero = jnp.zeros((128, 128), f32)
    for a in range(3):
        inverse = jnp.concatenate([s_ref[a, b] if b <= a else zero for b in range(3)], axis=1)
        by_row_ref[128 * a : 128 * a + 128, :] = dot(inverse, by_row, 1, 0)
        by_col_ref[128 * a : 128 * a + 128, :] = dot(inverse, by_col, 1, 0)


def update_kernel(col_ref, by_row_ref, by_col_ref, right_ref, left_ref, matrix_ref, out_ref):
    rows = matrix_ref.shape[0]
    left = dot(by_col_ref[...], left_ref[...], 1, 0)
    k = lax.broadcasted_iota(jnp.int32, (WIDTH, 128), 0)
    j = lax.broadcasted_iota(jnp.int32, (WIDTH, 128), 1)
    pick = jnp.where((k == j * N_COL + col_ref[0]) & (j < TILE_COLS), 1.0, 0.0).astype(f32)
    panel = dot(left, pick, 0, 0)
    i = lax.broadcasted_iota(jnp.int32, (WIDTH, rows), 1)
    k = lax.broadcasted_iota(jnp.int32, (WIDTH, rows), 0)
    half = TILE_ROWS // 2
    keep = (i < half) | ((i < TILE_ROWS) & (k >= PANEL))
    left = jnp.where(keep, 0.0, left)
    row = lax.broadcasted_iota(jnp.int32, (rows, 128), 0)
    lane = lax.broadcasted_iota(jnp.int32, (rows, 128), 1)
    in_panel = (lane < TILE_COLS // 2) | ((lane < TILE_COLS) & (row >= half))
    for b in range(4):
        cut = slice(256 * b, 256 * b + 256)
        right = dot(by_row_ref[...], right_ref[:, cut], 1, 0)
        value = matrix_ref[:, cut] - dot(left, right, 0, 0)
        if b == 0:
            out_ref[:, 0:128] = jnp.where(in_panel, panel, value[:, 0:128])
            out_ref[:, 128:256] = value[:, 128:256]
        else:
            out_ref[:, cut] = value


def per_device(matrix):
    local_rows, local_cols = matrix.shape
    top = matrix[:TILE_ROWS]
    right = lax.all_to_all(
        jnp.broadcast_to(top[None], (N_ROW, TILE_ROWS, local_cols)), "row", 0, 0
    ).reshape(WIDTH, local_cols)
    corner = lax.all_gather(right[:, :TILE_COLS].T, "col", axis=0, tiled=True)
    left = lax.all_gather(matrix[:, :TILE_COLS].T, "col", axis=0, tiled=True)
    square = jax.ShapeDtypeStruct((WIDTH, WIDTH), f32)
    by_row, by_col = pl.pallas_call(
        factor_kernel,
        out_shape=(square, square),
        scratch_shapes=[pltpu.VMEM((3, 3, 128, 128), f32)],
    )(corner)
    vmem = pl.BlockSpec(memory_space=pltpu.VMEM)
    return pl.pallas_call(
        update_kernel,
        out_shape=jax.ShapeDtypeStruct((local_rows, local_cols), f32),
        in_specs=[pl.BlockSpec(memory_space=pltpu.SMEM)] + [vmem] * 5,
        out_specs=vmem,
    )(lax.axis_index("col").reshape(1).astype(jnp.int32), by_row, by_col, right, left, matrix)


def solution(mesh):
    return jax.shard_map(
        per_device,
        mesh=mesh,
        in_specs=(P("row", "col"),),
        out_specs=P("row", "col"),
        check_vma=False,
    )
```

time: 631 us -> 129 us (0.20)
  waiting for transfers between devices: 298 us -> 20.9 us
  other arithmetic: 104 us -> 0 us
  blocking collectives: 158 us -> 56.1 us
  Pallas kernels: 0 us -> 36.6 us
  local copies, waits for them, and re-layouts: 39.9 us -> 4.89 us
  between operations: 16.5 us -> 0.03 us
  starting transfers between devices: 0.22 us -> 10.6 us
  matrix products: 10.1 us -> 0 us
    psum x2 -> x0, waiting for transfers between devices: 298 us -> none  [spread(): return lax.psum(block, axis)]
    another operation x30 -> x0, other arithmetic: 104 us -> none  [the longest x14 57.6 us: per_device(): lower_factor = jnp.linalg.cholesky(corner)]
    all_gather x6 -> x2, blocking collectives: 158 us -> 56.1 us  [the longest x1 28.6 us: per_device(): corner = lax.all_gather(right[:, :TILE_COLS].T, 'col', axis=0, tiled=True)]
    pallas_call x0 -> x2, Pallas kernels: none -> 36.6 us  [the longest x1 23.8 us: per_device(): pl.pallas_call(factor_kernel, out_shape=(square, square), scratch_shapes=...]
    scatter-add x3 -> x0, local copies, waits for them, and re-layouts: 23.4 us -> none  [per_device(): matrix = matrix.at[row_low:local_rows, col_low:local_cols].add(-term)]
    all_to_all x0 -> x1, waiting for transfers between devices: none -> 20.9 us  [per_device(): lax.all_to_all(jnp.broadcast_to(top[None], (N_ROW, TILE_ROWS, local_cols)...]
    all_to_all x0 -> x1, starting transfers between devices: none -> 10.6 us  [per_device(): lax.all_to_all(jnp.broadcast_to(top[None], (N_ROW, TILE_ROWS, local_cols)...]
    dot_general x2 -> x0, matrix products: 6.58 us -> none  [per_device(): jnp.dot(factor_left_rows[row_low:local_rows], factor_right_rows.T, precis...]
  transfers between devices with their start and end apart: 2 -> 1, of which waited for: 2 -> 1; matrix products, arithmetic and copies ran while one was open for 0% -> 0% of each run, Pallas kernels for 0% -> 0%
where the time goes in v1:
time: 129 us
  blocking collectives  56.1 us (43%)
  Pallas kernels  36.6 us (28%)
  waiting for transfers between devices  20.9 us (16%)
  starting transfers between devices  10.6 us (8%)
  local copies, waits for them, and re-layouts  4.89 us (4%)
    all_gather x1, blocking collectives, per_device(): corner = lax.all_gather(right[:, :TILE_COLS].T, 'col', axis=0, tiled=True)  28.6 us
    all_gather x1, blocking collectives, per_device(): left = lax.all_gather(matrix[:, :TILE_COLS].T, 'col', axis=0, tiled=True)  27.5 us
    pallas_call x1, Pallas kernels, per_device(): pl.pallas_call(factor_kernel, out_shape=(square, square), scratch_shapes=...  23.8 us
    all_to_all x1, waiting for transfers between devices, per_device(): lax.all_to_all(jnp.broadcast_to(top[None], (N_ROW, TILE_ROWS, local_cols)...  20.9 us
    pallas_call x1, Pallas kernels, per_device(): pl.pallas_call(update_kernel, out_shape=jax.ShapeDtypeStruct((local_rows,...  12.8 us
    all_to_all x1, starting transfers between devices, per_device(): lax.all_to_all(jnp.broadcast_to(top[None], (N_ROW, TILE_ROWS, local_cols)...  10.6 us
  transfers between devices with their start and end apart: 1, of which 1 were waited for; matrix products, arithmetic and copies ran while one was open for 0% of the time, Pallas kernels for 0%

profile of v1, /device:TPU:1, one launch (start us, length us, event | category | flops | bytes accessed | tf_op | source)
XLA Modules:
  0.0 129.1 jit_solution(5089800378080518068)
XLA Ops:
  0.0 0.8 slice.9
  0.8 1.6 %broadcast_in_dim.2 = f32[32,12,1024]{2,1,0:T(8,128)} broadcast(f32[12,1024]{1,0:T(8,128)S(1)} %slice.9), dimensions={1,2} | broadcast | bytes 1622016 | tf_op jit(solution)/shard_map/broadcast_in_dim | solution.py:163
  2.4 0.0 slice-start
  2.4 10.6 %all-to-all-start = ((f32[32,12,1024]{2,1,0:T(8,128)}), f32[32,12,1024]{2,1,0:T(8,128)S(1)}, u32[]{:S(2)}, u32[]{:S(2)}) async-start(f32[32,12,1024]{2,1,0:T(8,128)} %broadcast_in_dim.2), calls=%async_computation | async-start | bytes 4194304 | tf_op jit(solution)/shard_map/all_to_all | solution.py:162
  13.1 0.0 slice-done
  13.1 0.1 copy.7
  13.2 27.5 %all_gather.7.left_ref = f32[384,512]{1,0:T(8,128)} all-gather(f32[24,512]{1,0:T(8,128)S(1)} %bitcast.3), channel_id=1, replica_groups=mesh['row'=32,'col'=16] {'col'}, dimensions={0}, use_global_device_ids=true | all-gather | bytes 835584 | tf_op jit(solution)/shard_map/all_gather | solution.py:166
  40.7 20.9 %all-to-all-done = f32[32,12,1024]{2,1,0:T(8,128)S(1)} async-done(((f32[32,12,1024]{2,1,0:T(8,128)}), f32[32,12,1024]{2,1,0:T(8,128)S(1)}, u32[]{:S(2)}, u32[]{:S(2)}) %all-to-all-start) | async-done | bytes 1572896 | tf_op jit(solution)/shard_map/all_to_all | solution.py:162
  61.5 1.3 %reshape.8.right_ref = f32[384,1024]{1,0:T(8,128)} reshape(f32[32,12,1024]{2,1,0:T(8,128)S(1)} %all-to-all-done) | data formatting | bytes 3145728 | tf_op jit(solution)/shard_map/reshape | solution.py:164
  62.9 0.9 slice.12
  63.8 0.1 copy.6
  63.9 28.6 %all_gather.6.corner_ref = f32[384,384]{1,0:T(8,128)} all-gather(f32[24,384]{1,0:T(8,128)S(1)} %bitcast.4), channel_id=1, replica_groups=mesh['row'=32,'col'=16] {'col'}, dimensions={0}, use_global_device_ids=true | all-gather | bytes 626688 | tf_op jit(solution)/shard_map/all_gather | solution.py:165
  92.5 23.8 %shard_map.17 = (f32[384,384]{1,0:T(8,128)}, f32[384,384]{1,0:T(8,128)}) custom-call(f32[384,384]{1,0:T(8,128)} %all_gather.6.corner_ref), custom_call_target="tpu_custom_call" | custom-call | tf_op jit(solution)/shard_map/pallas_call | solution.py:168
  116.3 12.8 %shard_map.18 = f32[512,1024]{1,0:T(8,128)} custom-call(s32[1]{0:T(128)} %bitcast.col_ref, f32[384,384]{1,0:T(8,128)} %get-tuple-element.7.by_row_ref, f32[384,384]{1,0:T(8,128)} %get-tuple-element.8.by_col_ref, f32[384,1024]{1,0:T(8,128)} %reshape.8.right_ref, f32[384,512]{1,0:T(8,128)} %all_gather.7.left_ref, f32[512,1024]{1,0:T(8,128)} %matrix_ref.1), custom_call_target="tpu_custom_call" | custom-call | tf_op jit(solution)/shard_map/pallas_call | solution.py:174
Async XLA Ops:
  2.4 10.6 %slice-start = ((f32[512,1024]{1,0:T(8,128)}), f32[512,24]{1,0:T(8,128)S(1)}, s32[]{:S(2)}) async-start(f32[512,1024]{1,0:T(8,128)} %matrix_ref.1), calls=%async_computation.1 | async-start | bytes 524288 | tf_op jit(solution)/shard_map/slice | solution.py:166
  2.4 59.1 %all-to-all-start = ((f32[32,12,1024]{2,1,0:T(8,128)}), f32[32,12,1024]{2,1,0:T(8,128)S(1)}, u32[]{:S(2)}, u32[]{:S(2)}) async-start(f32[32,12,1024]{2,1,0:T(8,128)} %broadcast_in_dim.2), calls=%async_computation | async-start | bytes 4194304 | tf_op jit(solution)/shard_map/all_to_all | solution.py:162

commit v2 on v1

v2 whole, which is shorter than its diff:
```python
import jax
import jax.numpy as jnp
from jax import lax
from jax.experimental import pallas as pl
from jax.experimental.pallas import tpu as pltpu
from jax.sharding import PartitionSpec as P

PANEL = 192
WIDTH = 384
N_ROW = 32
N_COL = 16
TILE_ROWS = WIDTH // N_ROW
TILE_COLS = WIDTH // N_COL
f32 = jnp.float32


def dot(a, b, over_a, over_b):
    return lax.dot_general(
        a,
        b,
        (((over_a,), (over_b,)), ((), ())),
        precision=lax.Precision.HIGHEST,
        preferred_element_type=f32,
    )


def full(value):
    return jnp.broadcast_to(value, (8, 128))


def tree(values):
    values = list(values)
    while len(values) > 1:
        values = [
            values[i] + values[i + 1] if i + 1 < len(values) else values[i]
            for i in range(0, len(values), 2)
        ]
    return values[0]


def factor(block):
    block = list(block)
    count = len(block)
    lane = lax.broadcasted_iota(jnp.int32, (8, 128), 1)
    sub = lax.broadcasted_iota(jnp.int32, (8, 128), 0)
    for q in range(count):
        first = 8 * q
        cols = {
            (i, t): full(block[i][:, first + t : first + t + 1])
            for i in range(q, count)
            for t in range(8)
        }
        e = [[full(cols[q, t][s : s + 1, :]) if s >= t else None for t in range(8)] for s in range(8)]
        scale = [None] * 8
        low = [[None] * 8 for _ in range(8)]
        inv = [[None] * 8 for _ in range(8)]
        for t in range(8):
            scale[t] = lax.rsqrt(e[t][t])
            for s in range(t + 1, 8):
                low[s][t] = e[s][t] * scale[t]
            for u in range(t + 1, 8):
                for s in range(u, 8):
                    e[s][u] = e[s][u] - low[s][t] * low[u][t]
            inv[t][t] = scale[t]
            for u in range(t):
                inv[t][u] = -(tree([low[t][v] * inv[v][u] for v in range(u, t)]) * scale[t])
        here = (lane >= first) & (lane < first + 8)
        eye = jnp.where(lane - first == sub, 1.0, 0.0).astype(f32)
        own = jnp.where(here, eye, block[q])
        raw = [full(own[t : t + 1, :]) for t in range(8)]
        rows = [tree([inv[t][u] * raw[u] for u in range(t + 1)]) for t in range(8)]
        own = rows[0]
        for t in range(1, 8):
            own = jnp.where(sub == t, rows[t], own)
        block[q] = own
        if q + 1 < count:
            back = [tree([inv[u][t] * rows[u] for u in range(t, 8)]) for t in range(8)]
            for i in range(q + 1, count):
                block[i] = jnp.where(here, 0.0, block[i]) - tree(
                    [cols[i, t] * back[t] for t in range(8)]
                )
    return block


def pack_kernel(head_ref, out_ref):
    lane = lax.broadcasted_iota(jnp.int32, (1, 128), 1)
    for a in range(4):
        total = jnp.zeros((1, 128), f32)
        for b in range(4):
            i = 4 * a + b
            if i < TILE_ROWS:
                row = jnp.where(lane < TILE_COLS, head_ref[i : i + 1, :], 0.0)
                total = total + (pltpu.roll(row, 32 * b, 1) if b else row)
        out_ref[:, a, :] = jnp.broadcast_to(total, (N_ROW, 128))


def unpack_kernel(tile_ref, out_ref):
    for a in range(3):
        part = tile_ref[:, a, :]
        stack = jnp.concatenate(
            [part] + [pltpu.roll(part, 128 - 32 * b, 1) for b in range(1, 4)], axis=0
        )
        out_ref[:, 128 * a : 128 * a + 128] = jnp.transpose(stack)[:TILE_COLS]


def factor_kernel(corner_ref, out_ref, s_ref):
    for j in range(TILE_COLS):
        value = corner_ref[:, j, :]
        a, offset = j * N_COL // 128, j * N_COL % 128
        for b in range(a, 3):
            s_ref[a, b, offset : offset + N_COL, :] = value[:, 128 * b : 128 * b + 128]
    row = lax.broadcasted_iota(jnp.int32, (128, 128), 0)
    col = lax.broadcasted_iota(jnp.int32, (128, 128), 1)
    zero = jnp.zeros((128, 128), f32)
    s = {(a, b): s_ref[a, b] for a in range(3) for b in range(a, 3)}
    for p in range(3):
        block = factor([s[p, p][8 * i : 8 * i + 8, :] for i in range(16)])
        own = jnp.where(col <= row, jnp.concatenate(block, axis=0), 0.0)
        w = {b: dot(own, s[p, b], 1, 0) for b in range(3) if b != p}
        w[p] = own
        for b in range(3):
            out_ref[128 * p : 128 * p + 128, 128 * b : 128 * b + 128] = w[b] if b <= p else zero
        for a in range(p + 1, 3):
            for b in [b for b in (1, 2, 0) if b >= a or b <= p]:
                value = dot(w[a], w[b], 0, 0)
                s[a, b] = -value if b == p else s[a, b] - value


def split(value):
    high = value.astype(jnp.bfloat16)
    return high, (value - high.astype(f32)).astype(jnp.bfloat16)


def dot3(a, b, over_a, over_b):
    def one(x, y):
        return lax.dot_general(
            x, y, (((over_a,), (over_b,)), ((), ())), preferred_element_type=f32
        )

    return one(a[0], b[0]) + (one(a[0], b[1]) + one(a[1], b[0]))


def update_kernel(
    col_ref, inv_ref, right_ref, left_ref, matrix_ref, out_ref, rh_ref, rl_ref, lh_ref, ll_ref, panel_ref, ih_ref, il_ref
):
    rows = matrix_ref.shape[0]
    half = TILE_ROWS // 2
    block = pl.program_id(0)

    @pl.when(block == 0)
    def _():
        ih_ref[...], il_ref[...] = split(inv_ref[...])
        for j in range(TILE_COLS):
            cut = slice(N_COL * j, N_COL * j + N_COL)
            lh_ref[cut], ll_ref[cut] = split(left_ref[:, j, :])
        left = dot3((ih_ref[...], il_ref[...]), (lh_ref[...], ll_ref[...]), 1, 0)
        k = lax.broadcasted_iota(jnp.int32, (WIDTH, 128), 0)
        j = lax.broadcasted_iota(jnp.int32, (WIDTH, 128), 1)
        pick = jnp.where((k == j * N_COL + col_ref[0]) & (j < TILE_COLS), 1.0, 0.0).astype(f32)
        panel_ref[...] = dot(left, pick, 0, 0)
        i = lax.broadcasted_iota(jnp.int32, (WIDTH, rows), 1)
        k = lax.broadcasted_iota(jnp.int32, (WIDTH, rows), 0)
        keep = (i < half) | ((i < TILE_ROWS) & (k >= PANEL))
        lh_ref[...], ll_ref[...] = split(jnp.where(keep, 0.0, left))

    for i in range(TILE_ROWS):
        cut = slice(N_ROW * i, N_ROW * i + N_ROW)
        rh_ref[cut], rl_ref[cut] = split(right_ref[:, i, :])
    right = split(dot3((ih_ref[...], il_ref[...]), (rh_ref[...], rl_ref[...]), 1, 0))
    out_ref[...] = matrix_ref[...] - dot3((lh_ref[...], ll_ref[...]), right, 0, 0)

    @pl.when(block == 0)
    def _():
        row = lax.broadcasted_iota(jnp.int32, (rows, 128), 0)
        lane = lax.broadcasted_iota(jnp.int32, (rows, 128), 1)
        in_panel = (lane < TILE_COLS // 2) | ((lane < TILE_COLS) & (row >= half))
        out_ref[:, 0:128] = jnp.where(in_panel, panel_ref[...], out_ref[:, 0:128])


def replicated(value, count):
    return jnp.broadcast_to(value[None], (count,) + value.shape)


def per_device(matrix):
    local_rows, local_cols = matrix.shape
    packed = pl.pallas_call(
        pack_kernel,
        grid=(1,),
        in_specs=[pl.BlockSpec((16, 128), lambda g: (0, 0))],
        out_specs=pl.BlockSpec((N_ROW, 4, 128), lambda g: (0, 0, 0)),
        out_shape=jax.ShapeDtypeStruct((N_ROW, 4, 128), f32),
    )(matrix)
    left = lax.all_gather(matrix[:, :TILE_COLS].T, "col", axis=0)
    packed = lax.all_to_all(packed, "row", 0, 0)
    top = replicated(matrix[:TILE_ROWS], N_ROW)
    packed, left, top = lax.optimization_barrier((packed, left, top))
    right = lax.all_to_all(top, "row", 0, 0)
    tile = pl.pallas_call(
        unpack_kernel, out_shape=jax.ShapeDtypeStruct((TILE_COLS, WIDTH), f32)
    )(packed)
    corner = lax.all_gather(tile, "col", axis=0)
    inverse = pl.pallas_call(
        factor_kernel,
        out_shape=jax.ShapeDtypeStruct((WIDTH, WIDTH), f32),
        scratch_shapes=[pltpu.VMEM((3, 3, 128, 128), f32)],
    )(corner)
    step = 256
    bf16 = jnp.bfloat16
    return pl.pallas_call(
        update_kernel,
        grid=(local_cols // step,),
        out_shape=jax.ShapeDtypeStruct((local_rows, local_cols), f32),
        in_specs=[
            pl.BlockSpec(memory_space=pltpu.SMEM),
            pl.BlockSpec((WIDTH, WIDTH), lambda g: (0, 0)),
            pl.BlockSpec((N_ROW, TILE_ROWS, step), lambda g: (0, 0, g)),
            pl.BlockSpec((N_COL, TILE_COLS, local_rows), lambda g: (0, 0, 0)),
            pl.BlockSpec((local_rows, step), lambda g: (0, g)),
        ],
        out_specs=pl.BlockSpec((local_rows, step), lambda g: (0, g)),
        scratch_shapes=[pltpu.VMEM((WIDTH, step), bf16)] * 2
        + [pltpu.VMEM((WIDTH, local_rows), bf16)] * 2
        + [pltpu.VMEM((local_rows, 128), f32)]
        + [pltpu.VMEM((WIDTH, WIDTH), bf16)] * 2,
    )(lax.axis_index("col").reshape(1).astype(jnp.int32), inverse, right, left, matrix)


def solution(mesh):
    return jax.shard_map(
        per_device,
        mesh=mesh,
        in_specs=(P("row", "col"),),
        out_specs=P("row", "col"),
        check_vma=False,
    )
```

time: 129 us -> 118 us (0.915); the launches traced: 129 us -> 117 us
  blocking collectives: 56.1 us -> 45.3 us
  waiting for transfers between devices: 20.9 us -> 10.6 us
  starting transfers between devices: 10.6 us -> 20 us
  local copies, waits for them, and re-layouts: 4.89 us -> 3.02 us
    all_gather x2, blocking collectives: 56.1 us -> 45.3 us  [the longest x1 27.5 us: per_device(): left = lax.all_gather(matrix[:, :TILE_COLS].T, 'col', axis=0)]
    all_to_all x1 -> x2, waiting for transfers between devices: 20.9 us -> 10.6 us  [the longest x1 10.6 us: per_device(): right = lax.all_to_all(top, 'row', 0, 0)]
    all_to_all x1 -> x2, starting transfers between devices: 10.6 us -> 20 us  [the longest x1 10.5 us: per_device(): packed = lax.all_to_all(packed, 'row', 0, 0)]
    slice x4, local copies, waits for them, and re-layouts: 1.79 us -> 0.01 us  [the longest x2 0.01 us: per_device(): left = lax.all_gather(matrix[:, :TILE_COLS].T, 'col', axis=0)]
    reshape x1 -> x0, local copies, waits for them, and re-layouts: 1.34 us -> none  [per_device(): right = lax.all_to_all(jnp.broadcast_to(top[None], (N_ROW, TILE_ROWS, loc...]
    pallas_call x2 -> x4, Pallas kernels: 36.6 us -> 37.5 us  [the longest x1 18.2 us: per_device(): pl.pallas_call(factor_kernel, out_shape=jax.ShapeDtypeStruct((WIDTH, WIDT...]
  transfers between devices with their start and end apart: 1 -> 2, of which waited for: 1 -> 1; matrix products, arithmetic and copies ran while one was open for 0% -> 0% of each run, Pallas kernels for 0% -> 17%
where the time goes in v2:
time: 118 us; the launch traced here: 117 us
  blocking collectives  45.3 us (38%)
  Pallas kernels  37.5 us (32%)
  starting transfers between devices  20 us (17%)
  waiting for transfers between devices  10.6 us (9%)
  local copies, waits for them, and re-layouts  3.02 us (3%)
    all_gather x1, blocking collectives, per_device(): left = lax.all_gather(matrix[:, :TILE_COLS].T, 'col', axis=0)  27.5 us
    pallas_call x1, Pallas kernels, per_device(): pl.pallas_call(factor_kernel, out_shape=jax.ShapeDtypeStruct((WIDTH, WIDT...  18.2 us
    all_gather x1, blocking collectives, per_device(): corner = lax.all_gather(tile, 'col', axis=0)  17.9 us
    pallas_call x1, Pallas kernels, per_device(): pl.pallas_call(update_kernel, grid=(local_cols // step,), out_shape=jax.S...  16 us
    all_to_all x1, waiting for transfers between devices, per_device(): right = lax.all_to_all(top, 'row', 0, 0)  10.6 us
    all_to_all x1, starting transfers between devices, per_device(): packed = lax.all_to_all(packed, 'row', 0, 0)  10.5 us
    all_to_all x1, starting transfers between devices, per_device(): right = lax.all_to_all(top, 'row', 0, 0)  9.5 us
  transfers between devices with their start and end apart: 2, of which 1 were waited for; matrix products, arithmetic and copies ran while one was open for 0% of the time, Pallas kernels for 17%

profile of v2, /device:TPU:1, one launch (start us, length us, event | category | flops | bytes accessed | tf_op | source)
XLA Modules:
  0.0 116.5 jit_solution(15885090018941325535)
XLA Ops:
  0.0 0.0 slice-start
  0.0 0.0 slice-start.1
  0.0 1.6 %shard_map.17 = f32[32,4,128]{2,1,0:T(4,128)} custom-call(f32[512,1024]{1,0:T(8,128)} %matrix_ref.1), custom_call_target="tpu_custom_call" | custom-call | tf_op jit(solution)/shard_map/pallas_call | solution.py:186
  1.6 10.5 %all-to-all-start = ((f32[32,4,128]{2,1,0:T(4,128)}), f32[32,4,128]{2,1,0:T(4,128)S(1)}, u32[]{:S(2)}, u32[]{:S(2)}) async-start(f32[32,4,128]{2,1,0:T(4,128)} %shard_map.17), calls=%async_computation | async-start | bytes 131072 | tf_op jit(solution)/shard_map/all_to_all | solution.py:194
  12.1 0.0 slice-done
  12.1 0.1 copy.4
  12.2 27.5 %all-gather = f32[384,512]{1,0:T(8,128)} all-gather(f32[24,512]{1,0:T(8,128)S(1)} %bitcast.6), channel_id=2, replica_groups=mesh['row'=32,'col'=16] {'col'}, dimensions={0}, use_global_device_ids=true | all-gather | bytes 835584 | tf_op jit(solution)/shard_map/all_gather | solution.py:193
  39.7 0.0 all-to-all-done.tile_ref
  39.7 0.0 copy-start.1
  39.7 0.0 slice-done.1
  39.7 1.6 %broadcast_in_dim.2 = f32[32,12,1024]{2,1,0:T(8,128)} broadcast(f32[12,1024]{1,0:T(8,128)S(1)} %slice-done.1), dimensions={1,2} | broadcast | bytes 1622016 | tf_op jit(solution)/shard_map/broadcast_in_dim | solution.py:181
  41.3 0.0 copy-done.1
  41.3 9.5 %all-to-all-start.1 = ((f32[32,12,1024]{2,1,0:T(8,128)}), f32[32,12,1024]{2,1,0:T(8,128)S(1)}, u32[]{:S(2)}, u32[]{:S(2)}) async-start(f32[32,12,1024]{2,1,0:T(8,128)} %broadcast_in_dim.2), calls=%async_computation.1 | async-start | bytes 4194304 | tf_op jit(solution)/shard_map/all_to_all | solution.py:197
  50.8 1.7 %shard_map.18 = f32[24,384]{1,0:T(8,128)} custom-call(f32[32,4,128]{2,1,0:T(4,128)} %copy-done.1), custom_call_target="tpu_custom_call" | custom-call | tf_op jit(solution)/shard_map/pallas_call | solution.py:198
  52.5 17.9 %all-gather.1 = f32[384,384]{1,0:T(8,128)} all-gather(f32[24,384]{1,0:T(8,128)} %shard_map.18), channel_id=3, replica_groups=mesh['row'=32,'col'=16] {'col'}, dimensions={0}, use_global_device_ids=true | all-gather | bytes 626688 | tf_op jit(solution)/shard_map/all_gather | solution.py:201
  70.3 18.2 %shard_map.19.inv_ref = f32[384,384]{1,0:T(8,128)} custom-call(f32[16,24,384]{2,1,0:T(8,128)} %bitcast.5), custom_call_target="tpu_custom_call" | custom-call | tf_op jit(solution)/shard_map/pallas_call | solution.py:202
  88.5 10.6 %all-to-all-done.1.right_ref = f32[32,12,1024]{2,1,0:T(8,128)S(1)} async-done(((f32[32,12,1024]{2,1,0:T(8,128)}), f32[32,12,1024]{2,1,0:T(8,128)S(1)}, u32[]{:S(2)}, u32[]{:S(2)}) %all-to-all-start.1) | async-done | bytes 1572896 | tf_op jit(solution)/shard_map/all_to_all | solution.py:197
  99.2 0.0 copy-start
  99.2 1.3 %copy-done = f32[32,12,1024]{2,1,0:T(8,128)} copy-done((f32[32,12,1024]{2,1,0:T(8,128)}, f32[32,12,1024]{2,1,0:T(8,128)S(1)}, u32[]{:S(2)}) %copy-start) | copy-done | bytes 1572888
  100.5 16.0 %shard_map.20 = f32[512,1024]{1,0:T(8,128)} custom-call(s32[1]{0:T(128)} %bitcast.col_ref, f32[384,384]{1,0:T(8,128)} %shard_map.19.inv_ref, f32[32,12,1024]{2,1,0:T(8,128)} %copy-done, f32[16,24,512]{2,1,0:T(8,128)} %bitcast.4, f32[512,1024]{1,0:T(8,128)} %matrix_ref.1), custom_call_target="tpu_custom_call" | custom-call | tf_op jit(solution)/shard_map/pallas_call | solution.py:209
Async XLA Ops:
  0.0 12.1 %slice-start = ((f32[512,1024]{1,0:T(8,128)}), f32[512,24]{1,0:T(8,128)S(1)}, s32[]{:S(2)}) async-start(f32[512,1024]{1,0:T(8,128)} %matrix_ref.1), calls=%async_computation.2 | async-start | bytes 524288 | tf_op jit(solution)/shard_map/slice | solution.py:193
  0.0 39.7 %slice-start.1 = ((f32[512,1024]{1,0:T(8,128)}), f32[12,1024]{1,0:T(8,128)S(1)}, s32[]{:S(2)}) async-start(f32[512,1024]{1,0:T(8,128)} %matrix_ref.1), calls=%async_computation.3 | async-start | bytes 131072 | tf_op jit(solution)/shard_map/slice | solution.py:195
  1.6 38.1 %all-to-all-start = ((f32[32,4,128]{2,1,0:T(4,128)}), f32[32,4,128]{2,1,0:T(4,128)S(1)}, u32[]{:S(2)}, u32[]{:S(2)}) async-start(f32[32,4,128]{2,1,0:T(4,128)} %shard_map.17), calls=%async_computation | async-start | bytes 131072 | tf_op jit(solution)/shard_map/all_to_all | solution.py:194
  39.7 1.6 %copy-start.1 = (f32[32,4,128]{2,1,0:T(4,128)}, f32[32,4,128]{2,1,0:T(4,128)S(1)}, u32[]{:S(2)}) copy-start(f32[32,4,128]{2,1,0:T(4,128)S(1)} %all-to-all-done.tile_ref) | copy-start | bytes 196612
  41.3 57.9 %all-to-all-start.1 = ((f32[32,12,1024]{2,1,0:T(8,128)}), f32[32,12,1024]{2,1,0:T(8,128)S(1)}, u32[]{:S(2)}, u32[]{:S(2)}) async-start(f32[32,12,1024]{2,1,0:T(8,128)} %broadcast_in_dim.2), calls=%async_computation.1 | async-start | bytes 4194304 | tf_op jit(solution)/shard_map/all_to_all | solution.py:197
  99.2 1.3 %copy-start = (f32[32,12,1024]{2,1,0:T(8,128)}, f32[32,12,1024]{2,1,0:T(8,128)S(1)}, u32[]{:S(2)}) copy-start(f32[32,12,1024]{2,1,0:T(8,128)S(1)} %all-to-all-done.1.right_ref) | copy-start | bytes 4718596

commit v3 on v2

v3 whole, which is shorter than its diff:
```python
import jax
import jax.numpy as jnp
from jax import lax
from jax.experimental import pallas as pl
from jax.experimental.pallas import tpu as pltpu
from jax.sharding import PartitionSpec as P

PANEL = 192
WIDTH = 384
N_ROW = 32
N_COL = 16
TILE_ROWS = WIDTH // N_ROW
TILE_COLS = WIDTH // N_COL
f32 = jnp.float32


def dot(a, b, over_a, over_b):
    return lax.dot_general(
        a,
        b,
        (((over_a,), (over_b,)), ((), ())),
        precision=lax.Precision.HIGHEST,
        preferred_element_type=f32,
    )


def full(value):
    return jnp.broadcast_to(value, (8, 128))


def tree(values):
    values = list(values)
    while len(values) > 1:
        values = [
            values[i] + values[i + 1] if i + 1 < len(values) else values[i]
            for i in range(0, len(values), 2)
        ]
    return values[0]


def factor(block):
    block = list(block)
    count = len(block)
    lane = lax.broadcasted_iota(jnp.int32, (8, 128), 1)
    sub = lax.broadcasted_iota(jnp.int32, (8, 128), 0)
    for q in range(count):
        first = 8 * q
        cols = {
            (i, t): full(block[i][:, first + t : first + t + 1])
            for i in range(q, count)
            for t in range(8)
        }
        e = [[full(cols[q, t][s : s + 1, :]) if s >= t else None for t in range(8)] for s in range(8)]
        scale = [None] * 8
        low = [[None] * 8 for _ in range(8)]
        inv = [[None] * 8 for _ in range(8)]
        for t in range(8):
            scale[t] = lax.rsqrt(e[t][t])
            for s in range(t + 1, 8):
                low[s][t] = e[s][t] * scale[t]
            for u in range(t + 1, 8):
                for s in range(u, 8):
                    e[s][u] = e[s][u] - low[s][t] * low[u][t]
            inv[t][t] = scale[t]
            for u in range(t):
                inv[t][u] = -(tree([low[t][v] * inv[v][u] for v in range(u, t)]) * scale[t])
        here = (lane >= first) & (lane < first + 8)
        eye = jnp.where(lane - first == sub, 1.0, 0.0).astype(f32)
        own = jnp.where(here, eye, block[q])
        raw = [full(own[t : t + 1, :]) for t in range(8)]
        rows = [tree([inv[t][u] * raw[u] for u in range(t + 1)]) for t in range(8)]
        own = rows[0]
        for t in range(1, 8):
            own = jnp.where(sub == t, rows[t], own)
        block[q] = own
        if q + 1 < count:
            back = [tree([inv[u][t] * rows[u] for u in range(t, 8)]) for t in range(8)]
            for i in range(q + 1, count):
                block[i] = jnp.where(here, 0.0, block[i]) - tree(
                    [cols[i, t] * back[t] for t in range(8)]
                )
    return block


def split(value):
    high = value.astype(jnp.bfloat16)
    return high, (value - high.astype(f32)).astype(jnp.bfloat16)


def dot3(a, b, over_a, over_b):
    def one(x, y):
        return lax.dot_general(
            x, y, (((over_a,), (over_b,)), ((), ())), preferred_element_type=f32
        )

    return one(a[0], b[0]) + (one(a[0], b[1]) + one(a[1], b[0]))


def pack_kernel(head_ref, out_ref):
    lane = lax.broadcasted_iota(jnp.int32, (1, 128), 1)
    for a in range(4):
        total = jnp.zeros((1, 128), f32)
        for b in range(4):
            i = 4 * a + b
            if i < TILE_ROWS:
                row = jnp.where(lane < TILE_COLS, head_ref[i : i + 1, :], 0.0)
                total = total + (pltpu.roll(row, 32 * b, 1) if b else row)
        out_ref[:, a, :] = jnp.broadcast_to(total, (N_ROW, 128))


def unpack_kernel(tile_ref, out_ref):
    for a in range(3):
        part = tile_ref[pl.ds(a, N_ROW, stride=4), :]
        stack = jnp.concatenate(
            [part] + [pltpu.roll(part, 128 - 32 * b, 1) for b in range(1, 4)], axis=0
        )
        out_ref[TILE_COLS * a : TILE_COLS * a + TILE_COLS, :] = jnp.transpose(stack)[:TILE_COLS]


def factor_kernel(corner_ref, high_ref, rest_ref, s_ref):
    for j in range(TILE_COLS):
        a, offset = j * N_COL // 128, j * N_COL % 128
        for b in range(a, 3):
            s_ref[a, b, offset : offset + N_COL, :] = corner_ref[
                pl.ds(TILE_COLS * b + j, N_COL, stride=3 * TILE_COLS), :
            ]
    row = lax.broadcasted_iota(jnp.int32, (128, 128), 0)
    col = lax.broadcasted_iota(jnp.int32, (128, 128), 1)
    zero = jnp.zeros((128, 128), f32)
    s = {(a, b): s_ref[a, b] for a in range(3) for b in range(a, 3)}
    for p in range(3):
        block = factor([s[p, p][8 * i : 8 * i + 8, :] for i in range(16)])
        own = jnp.where(col <= row, jnp.concatenate(block, axis=0), 0.0)
        w = {b: dot(own, s[p, b], 1, 0) for b in range(3) if b != p}
        w[p] = own
        for b in range(3):
            at = (slice(128 * p, 128 * p + 128), slice(128 * b, 128 * b + 128))
            high_ref[at], rest_ref[at] = split(w[b] if b <= p else zero)
        for a in range(p + 1, 3):
            for b in [b for b in (1, 2, 0) if b >= a or b <= p]:
                value = dot(w[a], w[b], 0, 0)
                s[a, b] = -value if b == p else s[a, b] - value


def spread_kernel(head_ref, out_ref):
    chunks = out_ref.shape[1] // TILE_ROWS
    top = jnp.concatenate(
        [head_ref[:TILE_ROWS, 128 * b : 128 * b + 128] for b in range(chunks)], axis=0
    )
    for r in range(N_ROW):
        out_ref[r] = top


def turn_kernel(side_ref, out_ref):
    for b in range(side_ref.shape[0] // 128):
        part = jnp.transpose(side_ref[128 * b : 128 * b + 128, :])
        out_ref[TILE_COLS * b : TILE_COLS * b + TILE_COLS, :] = part[:TILE_COLS]


def left_kernel(col_ref, high_ref, rest_ref, left_ref, qh_ref, ql_ref, panel_ref, s_ref):
    rows = panel_ref.shape[0]
    half = TILE_ROWS // 2
    for j in range(TILE_COLS):
        for b in range(rows // 128):
            s_ref[N_COL * j : N_COL * j + N_COL, 128 * b : 128 * b + 128] = left_ref[
                pl.ds(TILE_COLS * b + j, N_COL, stride=TILE_COLS * rows // 128), :
            ]
    left = split(jnp.transpose(s_ref[...]))
    value = dot3(left, (high_ref[...], rest_ref[...]), 1, 1)
    k = lax.broadcasted_iota(jnp.int32, (WIDTH, 128), 0)
    j = lax.broadcasted_iota(jnp.int32, (WIDTH, 128), 1)
    pick = jnp.where((k == j * N_COL + col_ref[0]) & (j < TILE_COLS), 1.0, 0.0).astype(jnp.bfloat16)
    high, rest = split(value)
    panel_ref[...] = jnp.dot(high, pick, preferred_element_type=f32) + jnp.dot(
        rest, pick, preferred_element_type=f32
    )
    qh_ref[...] = high
    ql_ref[...] = rest
    i = lax.broadcasted_iota(jnp.int32, (16, WIDTH), 0)
    k = lax.broadcasted_iota(jnp.int32, (16, WIDTH), 1)
    keep = (i < half) | ((i < TILE_ROWS) & (k >= PANEL))
    qh_ref[:16, :], ql_ref[:16, :] = split(jnp.where(keep, 0.0, value[:16, :]))


def update_kernel(
    high_ref, rest_ref, qh_ref, ql_ref, panel_ref, right_ref, matrix_ref, out_ref, rh_ref, rl_ref
):
    rows = matrix_ref.shape[0]
    half = TILE_ROWS // 2
    block = pl.program_id(0)
    chunks = rh_ref.shape[1] // 128
    stride = right_ref.shape[0] // N_ROW
    for b in range(chunks):
        lanes = slice(128 * b, 128 * b + 128)
        for i in range(TILE_ROWS):
            cut = slice(N_ROW * i, N_ROW * i + N_ROW)
            first = (block * chunks + b) * TILE_ROWS + i
            rh_ref[cut, lanes], rl_ref[cut, lanes] = split(
                right_ref[pl.ds(first, N_ROW, stride=stride), :]
            )
    right = split(dot3((high_ref[...], rest_ref[...]), (rh_ref[...], rl_ref[...]), 1, 0))
    out_ref[...] = matrix_ref[...] - dot3((qh_ref[...], ql_ref[...]), right, 1, 0)

    @pl.when(block == 0)
    def _():
        row = lax.broadcasted_iota(jnp.int32, (rows, 128), 0)
        lane = lax.broadcasted_iota(jnp.int32, (rows, 128), 1)
        in_panel = (lane < TILE_COLS // 2) | ((lane < TILE_COLS) & (row >= half))
        out_ref[:, 0:128] = jnp.where(in_panel, panel_ref[...], out_ref[:, 0:128])


def finish(col, high, rest, left, right, matrix):
    local_rows, local_cols = matrix.shape
    bf16 = jnp.bfloat16
    vmem = pl.BlockSpec(memory_space=pltpu.VMEM)
    qh, ql, panel = pl.pallas_call(
        left_kernel,
        in_specs=[pl.BlockSpec(memory_space=pltpu.SMEM)] + [vmem] * 3,
        out_shape=(
            jax.ShapeDtypeStruct((local_rows, WIDTH), bf16),
            jax.ShapeDtypeStruct((local_rows, WIDTH), bf16),
            jax.ShapeDtypeStruct((local_rows, 128), f32),
        ),
        scratch_shapes=[pltpu.VMEM((WIDTH, local_rows), f32)],
    )(col, high, rest, left)
    step = 256
    whole = lambda g: (0, 0)
    return pl.pallas_call(
        update_kernel,
        grid=(local_cols // step,),
        out_shape=jax.ShapeDtypeStruct((local_rows, local_cols), f32),
        in_specs=[
            pl.BlockSpec((WIDTH, WIDTH), whole),
            pl.BlockSpec((WIDTH, WIDTH), whole),
            pl.BlockSpec((local_rows, WIDTH), whole),
            pl.BlockSpec((local_rows, WIDTH), whole),
            pl.BlockSpec((local_rows, 128), whole),
            pl.BlockSpec(right.shape, whole),
            pl.BlockSpec((local_rows, step), lambda g: (0, g)),
        ],
        out_specs=pl.BlockSpec((local_rows, step), lambda g: (0, g)),
        scratch_shapes=[pltpu.VMEM((WIDTH, step), bf16)] * 2,
    )(high, rest, qh, ql, panel, right, matrix)


def per_device(matrix):
    local_rows, local_cols = matrix.shape
    packed = pl.pallas_call(
        pack_kernel,
        grid=(1,),
        in_specs=[pl.BlockSpec((16, 128), lambda g: (0, 0))],
        out_specs=pl.BlockSpec((N_ROW, 4, 128), lambda g: (0, 0, 0)),
        out_shape=jax.ShapeDtypeStruct((N_ROW, 4, 128), f32),
    )(matrix)
    packed = lax.all_to_all(packed, "row", 0, 0)
    folded = (N_ROW, TILE_ROWS * local_cols // 128, 128)
    top = pl.pallas_call(
        spread_kernel,
        grid=(1,),
        in_specs=[pl.BlockSpec((16, local_cols), lambda g: (0, 0))],
        out_specs=pl.BlockSpec(folded, lambda g: (0, 0, 0)),
        out_shape=jax.ShapeDtypeStruct(folded, f32),
    )(matrix)
    tall = (TILE_COLS * local_rows // 128, 128)
    turned = pl.pallas_call(
        turn_kernel,
        grid=(1,),
        in_specs=[pl.BlockSpec((local_rows, 128), lambda g: (0, 0))],
        out_specs=pl.BlockSpec(tall, lambda g: (0, 0)),
        out_shape=jax.ShapeDtypeStruct(tall, f32),
    )(matrix)
    packed, top, turned = lax.optimization_barrier((packed, top, turned))
    right = lax.all_to_all(top, "row", 0, 0).reshape(-1, 128)
    tile = pl.pallas_call(
        unpack_kernel, out_shape=jax.ShapeDtypeStruct((3 * TILE_COLS, 128), f32)
    )(packed.reshape(N_ROW * 4, 128))
    corner = lax.all_gather(tile, "col", axis=0, tiled=True)
    corner, turned = lax.optimization_barrier((corner, turned))
    left = lax.all_gather(turned, "col", axis=0, tiled=True)
    square = jax.ShapeDtypeStruct((WIDTH, WIDTH), jnp.bfloat16)
    high, rest = pl.pallas_call(
        factor_kernel,
        out_shape=(square, square),
        scratch_shapes=[pltpu.VMEM((3, 3, 128, 128), f32)],
    )(corner)
    col = lax.axis_index("col").reshape(1).astype(jnp.int32)
    return finish(col, high, rest, left, right, matrix)


def solution(mesh):
    return jax.shard_map(
        per_device,
        mesh=mesh,
        in_specs=(P("row", "col"),),
        out_specs=P("row", "col"),
        check_vma=False,
    )
```

time: 118 us -> 106 us (0.90); the launches traced: 117 us -> 106 us
  waiting for transfers between devices: 10.6 us -> 4.99 us
  starting transfers between devices: 20 us -> 14.9 us
  local copies, waits for them, and re-layouts: 3.02 us -> 1.16 us
  Pallas kernels: 37.5 us -> 38.7 us
    all_to_all x1, waiting for transfers between devices: 10.6 us -> 0.01 us  [per_device(): right = lax.all_to_all(top, 'row', 0, 0).reshape(-1, 128)]
    all_to_all x1, starting transfers between devices: 9.5 us -> 4.37 us  [per_device(): right = lax.all_to_all(top, 'row', 0, 0).reshape(-1, 128)]
    all_to_all x1, waiting for transfers between devices: 0.01 us -> 4.98 us  [per_device(): packed = lax.all_to_all(packed, 'row', 0, 0)]
    broadcast_in_dim x1 -> x0, local copies, waits for them, and re-layouts: 1.57 us -> none  [replicated(): return jnp.broadcast_to(value[None], (count,) + value.shape)]
    pallas_call x3 -> x6, Pallas kernels: 35.9 us -> 37.2 us  [the longest x1 18.1 us: per_device(): pl.pallas_call(factor_kernel, out_shape=(square, square), scratch_shapes=...]
  transfers between devices with their start and end apart: 2 -> 2, of which waited for: 1 -> 1; matrix products, arithmetic and copies ran while one was open for 0% -> 0% of each run, Pallas kernels for 17% -> 26%
where the time goes in v3:
time: 106 us
  blocking collectives  46.1 us (43%)
  Pallas kernels  38.7 us (37%)
  starting transfers between devices  14.9 us (14%)
  waiting for transfers between devices  4.99 us (5%)
  local copies, waits for them, and re-layouts  1.16 us (1%)
    all_gather x1, blocking collectives, per_device(): corner = lax.all_gather(tile, 'col', axis=0, tiled=True)  27.9 us
    all_gather x1, blocking collectives, per_device(): left = lax.all_gather(turned, 'col', axis=0, tiled=True)  18.2 us
    pallas_call x1, Pallas kernels, per_device(): pl.pallas_call(factor_kernel, out_shape=(square, square), scratch_shapes=...  18.1 us
    all_to_all x1, starting transfers between devices, per_device(): packed = lax.all_to_all(packed, 'row', 0, 0)  10.5 us
    pallas_call x1, Pallas kernels, finish(): pl.pallas_call(update_kernel, grid=(local_cols // step,), out_shape=jax.S...  9.94 us
    all_to_all x1, waiting for transfers between devices, per_device(): packed = lax.all_to_all(packed, 'row', 0, 0)  4.98 us
    all_to_all x1, starting transfers between devices, per_device(): right = lax.all_to_all(top, 'row', 0, 0).reshape(-1, 128)  4.37 us
    pallas_call x1, Pallas kernels, finish(): pl.pallas_call(left_kernel, in_specs=[pl.BlockSpec(memory_space=pltpu.SME...  3.68 us
  transfers between devices with their start and end apart: 2, of which 1 were waited for; matrix products, arithmetic and copies ran while one was open for 0% of the time, Pallas kernels for 26%

profile of v3, /device:TPU:1, one launch (start us, length us, event | category | flops | bytes accessed | tf_op | source)
XLA Modules:
  0.0 105.8 jit_solution(7125874129660316873)
XLA Ops:
  0.0 1.4 %shard_map.17 = f32[32,4,128]{2,1,0:T(4,128)} custom-call(f32[512,1024]{1,0:T(8,128)} %matrix_ref.1), custom_call_target="tpu_custom_call" | custom-call | tf_op jit(solution)/shard_map/pallas_call | solution.py:248
  1.4 10.5 %all-to-all-start = ((f32[32,4,128]{2,1,0:T(4,128)}), f32[32,4,128]{2,1,0:T(4,128)S(1)}, u32[]{:S(2)}, u32[]{:S(2)}) async-start(f32[32,4,128]{2,1,0:T(4,128)} %shard_map.17), calls=%async_computation | async-start | bytes 131072 | tf_op jit(solution)/shard_map/all_to_all | solution.py:255
  11.9 1.7 %shard_map.19 = f32[96,128]{1,0:T(8,128)} custom-call(f32[512,1024]{1,0:T(8,128)} %matrix_ref.1), custom_call_target="tpu_custom_call" | custom-call | tf_op jit(solution)/shard_map/pallas_call | solution.py:265
  13.6 2.2 %shard_map.18 = f32[32,96,128]{2,1,0:T(8,128)} custom-call(f32[512,1024]{1,0:T(8,128)} %matrix_ref.1), custom_call_target="tpu_custom_call" | custom-call | tf_op jit(solution)/shard_map/pallas_call | solution.py:257
  15.8 0.0 copy-start.2
  15.8 5.0 %all-to-all-done = f32[32,4,128]{2,1,0:T(4,128)S(1)} async-done(((f32[32,4,128]{2,1,0:T(4,128)}), f32[32,4,128]{2,1,0:T(4,128)S(1)}, u32[]{:S(2)}, u32[]{:S(2)}) %all-to-all-start) | async-done | bytes 65568 | tf_op jit(solution)/shard_map/all_to_all | solution.py:255
  20.8 0.0 copy-start.1
  20.8 4.4 %all-to-all-start.1 = ((f32[32,96,128]{2,1,0:T(8,128)}), f32[32,96,128]{2,1,0:T(8,128)S(1)}, u32[]{:S(2)}, u32[]{:S(2)}) async-start(f32[32,96,128]{2,1,0:T(8,128)} %shard_map.18), calls=%async_computation.1 | async-start | bytes 3145728 | tf_op jit(solution)/shard_map/all_to_all | solution.py:273
  25.1 0.0 copy-done.1
  25.1 1.7 %shard_map.20 = f32[72,128]{1,0:T(8,128)} custom-call(f32[128,128]{1,0:T(8,128)} %bitcast.4), custom_call_target="tpu_custom_call" | custom-call | tf_op jit(solution)/shard_map/pallas_call | solution.py:274
  26.8 27.9 %all_gather.6.corner_ref = f32[1152,128]{1,0:T(8,128)} all-gather(f32[72,128]{1,0:T(8,128)} %shard_map.20), channel_id=1, replica_groups=mesh['row'=32,'col'=16] {'col'}, dimensions={0}, use_global_device_ids=true | all-gather | bytes 626688 | tf_op jit(solution)/shard_map/all_gather | solution.py:277
  54.8 18.1 %shard_map.21 = (bf16[384,384]{1,0:T(8,128)(2,1)}, bf16[384,384]{1,0:T(8,128)(2,1)}) custom-call(f32[1152,128]{1,0:T(8,128)} %all_gather.6.corner_ref), custom_call_target="tpu_custom_call" | custom-call | tf_op jit(solution)/shard_map/pallas_call | solution.py:281
  72.9 0.0 copy-done.2
  72.9 18.2 %all_gather.7.left_ref = f32[1536,128]{1,0:T(8,128)} all-gather(f32[96,128]{1,0:T(8,128)S(1)} %copy-done.2), channel_id=1, replica_groups=mesh['row'=32,'col'=16] {'col'}, dimensions={0}, use_global_device_ids=true | all-gather | bytes 835584 | tf_op jit(solution)/shard_map/all_gather | solution.py:279
  91.1 3.7 %shard_map.22 = (bf16[512,384]{1,0:T(8,128)(2,1)}, bf16[512,384]{1,0:T(8,128)(2,1)}, f32[512,128]{1,0:T(8,128)}) custom-call(s32[1]{0:T(128)} %bitcast.1.col_ref, bf16[384,384]{1,0:T(8,128)(2,1)} %get-tuple-element.18.high_ref, bf16[384,384]{1,0:T(8,128)(2,1)} %get-tuple-element.19.rest_ref, f32[1536,128]{1,0:T(8,128)} %all_gather.7.left_ref), custom_call_target="tpu_custom_call" | custom-call | tf_op jit(solution)/shard_map/pallas_call | solution.py:216
  94.7 0.0 all-to-all-done.1
  94.8 0.0 copy-start
  94.8 1.1 %copy-done = f32[32,96,128]{2,1,0:T(8,128)} copy-done((f32[32,96,128]{2,1,0:T(8,128)}, f32[32,96,128]{2,1,0:T(8,128)S(1)}, u32[]{:S(2)}) %copy-start) | copy-done | bytes 1572888
  95.9 9.9 %shard_map.23 = f32[512,1024]{1,0:T(8,128)} custom-call(bf16[384,384]{1,0:T(8,128)(2,1)} %get-tuple-element.18.high_ref, bf16[384,384]{1,0:T(8,128)(2,1)} %get-tuple-element.19.rest_ref, bf16[512,384]{1,0:T(8,128)(2,1)} %get-tuple-element.21.qh_ref, bf16[512,384]{1,0:T(8,128)(2,1)} %get-tuple-element.22.ql_ref, f32[512,128]{1,0:T(8,128)} %get-tuple-element.23.panel_ref, ...), custom_call_target="tpu_custom_call" | custom-call | tf_op jit(solution)/shard_map/pallas_call | solution.py:228
Async XLA Ops:
  1.4 19.3 %all-to-all-start = ((f32[32,4,128]{2,1,0:T(4,128)}), f32[32,4,128]{2,1,0:T(4,128)S(1)}, u32[]{:S(2)}, u32[]{:S(2)}) async-start(f32[32,4,128]{2,1,0:T(4,128)} %shard_map.17), calls=%async_computation | async-start | bytes 131072 | tf_op jit(solution)/shard_map/all_to_all | solution.py:255
  15.8 57.1 %copy-start.2 = (f32[96,128]{1,0:T(8,128)S(1)}, f32[96,128]{1,0:T(8,128)}, u32[]{:S(2)}) copy-start(f32[96,128]{1,0:T(8,128)} %shard_map.19) | copy-start | bytes 147460
  20.8 4.4 %copy-start.1 = (f32[32,4,128]{2,1,0:T(4,128)}, f32[32,4,128]{2,1,0:T(4,128)S(1)}, u32[]{:S(2)}) copy-start(f32[32,4,128]{2,1,0:T(4,128)S(1)} %all-to-all-done) | copy-start | bytes 196612
  20.8 74.0 %all-to-all-start.1 = ((f32[32,96,128]{2,1,0:T(8,128)}), f32[32,96,128]{2,1,0:T(8,128)S(1)}, u32[]{:S(2)}, u32[]{:S(2)}) async-start(f32[32,96,128]{2,1,0:T(8,128)} %shard_map.18), calls=%async_computation.1 | async-start | bytes 3145728 | tf_op jit(solution)/shard_map/all_to_all | solution.py:273
  94.8 1.1 %copy-start = (f32[32,96,128]{2,1,0:T(8,128)}, f32[32,96,128]{2,1,0:T(8,128)S(1)}, u32[]{:S(2)}) copy-start(f32[32,96,128]{2,1,0:T(8,128)S(1)} %all-to-all-done.1) | copy-start | bytes 4718596

commit v4 on v3

v4 whole, which is shorter than its diff:
```python
import jax
import jax.numpy as jnp
from jax import lax
from jax.experimental import pallas as pl
from jax.experimental.pallas import tpu as pltpu
from jax.sharding import PartitionSpec as P

PANEL = 192
WIDTH = 384
N_ROW = 32
N_COL = 16
TILE_ROWS = WIDTH // N_ROW
TILE_COLS = WIDTH // N_COL
f32 = jnp.float32


def dot(a, b, over_a, over_b):
    return lax.dot_general(
        a,
        b,
        (((over_a,), (over_b,)), ((), ())),
        precision=lax.Precision.HIGHEST,
        preferred_element_type=f32,
    )


def full(value):
    return jnp.broadcast_to(value, (8, 128))


def tree(values):
    values = list(values)
    while len(values) > 1:
        values = [
            values[i] + values[i + 1] if i + 1 < len(values) else values[i]
            for i in range(0, len(values), 2)
        ]
    return values[0]


def factor(block):
    block = list(block)
    count = len(block)
    lane = lax.broadcasted_iota(jnp.int32, (8, 128), 1)
    sub = lax.broadcasted_iota(jnp.int32, (8, 128), 0)

    def column(i, j):
        return full(block[i][:, j : j + 1])

    diag = [column(0, u) for u in range(8)]
    for q in range(count):
        first = 8 * q
        cols = {(i, t): column(i, first + t) for i in range(q + 1, count) for t in range(8)}
        if q + 1 < count:
            ahead = [column(q + 1, first + 8 + u) for u in range(8)]
        e = [[full(diag[t][s : s + 1, :]) if s >= t else None for t in range(8)] for s in range(8)]
        scale = [None] * 8
        low = [[None] * 8 for _ in range(8)]
        for t in range(8):
            scale[t] = lax.rsqrt(e[t][t])
            for s in range(t + 1, 8):
                low[s][t] = e[s][t] * scale[t]
            for u in range(t + 1, 8):
                for s in range(u, 8):
                    e[s][u] = e[s][u] - low[s][t] * low[u][t]
        here = (lane >= first) & (lane < first + 8)
        eye = jnp.where(lane - first == sub, 1.0, 0.0).astype(f32)
        own = jnp.where(here, eye, block[q])
        if q + 1 < count:
            done = []
            for t in range(8):
                value = cols[q + 1, t]
                for u in range(t):
                    value = value - low[t][u] * done[u]
                done.append(value * scale[t])
            diag = []
            for u in range(8):
                terms = [done[t] * full(done[t][u : u + 1, :]) for t in range(8)]
                diag.append((ahead[u] - tree(terms[:7])) - terms[7])
        rows = []
        for t in range(8):
            value = full(own[t : t + 1, :])
            for u in range(t):
                value = value - low[t][u] * rows[u]
            rows.append(value * scale[t])
        own = rows[0]
        for t in range(1, 8):
            own = jnp.where(sub == t, rows[t], own)
        block[q] = own
        if q + 1 < count:
            back = [None] * 8
            for t in reversed(range(8)):
                value = rows[t]
                for u in range(t + 1, 8):
                    value = value - low[u][t] * back[u]
                back[t] = value * scale[t]
            for i in range(q + 1, count):
                block[i] = jnp.where(here, 0.0, block[i]) - tree(
                    [cols[i, t] * back[t] for t in range(8)]
                )
    return block


def split(value):
    high = value.astype(jnp.bfloat16)
    return high, (value - high.astype(f32)).astype(jnp.bfloat16)


def narrow_dot(a, b, over_a, over_b):
    return lax.dot_general(a, b, (((over_a,), (over_b,)), ((), ())), preferred_element_type=f32)


def put(ref, rows, lanes, value, stacked):
    high, rest = split(value)
    parts = (high, rest, high) if stacked else (high, high, rest)
    for n in range(3):
        if stacked:
            ref[WIDTH * n + rows.start : WIDTH * n + rows.stop, lanes] = parts[n]
        else:
            ref[rows, WIDTH * n + lanes.start : WIDTH * n + lanes.stop] = parts[n]


def pack_kernel(head_ref, out_ref):
    lane = lax.broadcasted_iota(jnp.int32, (1, 128), 1)
    for a in range(4):
        total = jnp.zeros((1, 128), f32)
        for b in range(4):
            i = 4 * a + b
            if i < TILE_ROWS:
                row = jnp.where(lane < TILE_COLS, head_ref[i : i + 1, :], 0.0)
                total = total + (pltpu.roll(row, 32 * b, 1) if b else row)
        out_ref[:, a, :] = jnp.broadcast_to(total, (N_ROW, 128))


def unpack_kernel(tile_ref, out_ref):
    for a in range(3):
        part = tile_ref[pl.ds(a, N_ROW, stride=4), :]
        stack = jnp.concatenate(
            [part] + [pltpu.roll(part, 128 - 32 * b, 1) for b in range(1, 4)], axis=0
        )
        count = 8 * (a + 1)
        out_ref[4 * a * (a + 1) : 4 * a * (a + 1) + count, :] = jnp.transpose(stack)[:count]


def factor_kernel(corner_ref, out_ref, s_ref):
    for j in range(TILE_COLS):
        a, offset = j * N_COL // 128, j * N_COL % 128
        for b in range(a, 3):
            s_ref[a, b, offset : offset + N_COL, :] = corner_ref[
                pl.ds(4 * b * (b + 1) + j, N_COL, stride=2 * TILE_COLS), :
            ]
    row = lax.broadcasted_iota(jnp.int32, (128, 128), 0)
    col = lax.broadcasted_iota(jnp.int32, (128, 128), 1)
    zero = jnp.zeros((128, 128), f32)
    s = {(a, b): s_ref[a, b] for a in range(3) for b in range(a, 3)}
    for p in range(3):
        block = factor([s[p, p][8 * i : 8 * i + 8, :] for i in range(16)])
        own = jnp.where(col <= row, jnp.concatenate(block, axis=0), 0.0)
        w = {b: dot(own, s[p, b], 1, 0) for b in range(3) if b != p}
        w[p] = own
        for b in range(3):
            at = slice(128 * p, 128 * p + 128), slice(128 * b, 128 * b + 128)
            put(out_ref, *at, w[b] if b <= p else zero, False)
        for a in range(p + 1, 3):
            for b in [b for b in (1, 2, 0) if b >= a or b <= p]:
                value = dot(w[a], w[b], 0, 0)
                s[a, b] = -value if b == p else s[a, b] - value


def spread_kernel(head_ref, out_ref):
    chunks = out_ref.shape[1] // TILE_ROWS
    top = jnp.concatenate(
        [head_ref[:TILE_ROWS, 128 * b : 128 * b + 128] for b in range(chunks)], axis=0
    )
    for r in range(N_ROW):
        out_ref[r] = top


def turn_kernel(side_ref, out_ref):
    for b in range(side_ref.shape[0] // 128):
        part = jnp.transpose(side_ref[128 * b : 128 * b + 128, :])
        out_ref[TILE_COLS * b : TILE_COLS * b + TILE_COLS, :] = part[:TILE_COLS]


def left_product(col_ref, inv_ref, left_ref, q_ref, panel_ref, s_ref, t_ref):
    rows = panel_ref.shape[0]
    half = TILE_ROWS // 2
    for j in range(TILE_COLS):
        for b in range(rows // 128):
            s_ref[N_COL * j : N_COL * j + N_COL, 128 * b : 128 * b + 128] = left_ref[
                pl.ds(TILE_COLS * b + j, N_COL, stride=TILE_COLS * rows // 128), :
            ]
    every = slice(0, WIDTH)
    put(t_ref, slice(0, rows), every, jnp.transpose(s_ref[...]), False)
    high = inv_ref[:, 0:WIDTH]
    rest = inv_ref[:, 2 * WIDTH : 3 * WIDTH]
    value = narrow_dot(t_ref[...], jnp.concatenate([high, rest, high], axis=1), 1, 1)
    k = lax.broadcasted_iota(jnp.int32, (WIDTH, 128), 0)
    j = lax.broadcasted_iota(jnp.int32, (WIDTH, 128), 1)
    pick = jnp.where((k == j * N_COL + col_ref[0]) & (j < TILE_COLS), 1.0, 0.0).astype(jnp.bfloat16)
    high, rest = split(value)
    panel_ref[...] = narrow_dot(high, pick, 1, 0) + narrow_dot(rest, pick, 1, 0)
    put(q_ref, slice(0, rows), every, value, False)
    i = lax.broadcasted_iota(jnp.int32, (16, WIDTH), 0)
    k = lax.broadcasted_iota(jnp.int32, (16, WIDTH), 1)
    keep = (i < half) | ((i < TILE_ROWS) & (k >= PANEL))
    put(q_ref, slice(0, 16), every, jnp.where(keep, 0.0, value[:16, :]), False)


def update_kernel(
    col_ref, inv_ref, left_ref, right_ref, matrix_ref, out_ref, r_ref, u_ref, q_ref, panel_ref, s_ref, t_ref
):
    rows = matrix_ref.shape[0]
    half = TILE_ROWS // 2
    block = pl.program_id(0)

    @pl.when(block == 0)
    def _():
        left_product(col_ref, inv_ref, left_ref, q_ref, panel_ref, s_ref, t_ref)

    chunks = r_ref.shape[1] // 128
    stride = right_ref.shape[0] // N_ROW
    for b in range(chunks):
        for i in range(TILE_ROWS):
            first = (block * chunks + b) * TILE_ROWS + i
            put(
                r_ref,
                slice(N_ROW * i, N_ROW * i + N_ROW),
                slice(128 * b, 128 * b + 128),
                right_ref[pl.ds(first, N_ROW, stride=stride), :],
                True,
            )
    value = narrow_dot(inv_ref[...], r_ref[...], 1, 0)
    put(u_ref, slice(0, WIDTH), slice(0, 128 * chunks), value, True)
    out_ref[...] = matrix_ref[...] - narrow_dot(q_ref[...], u_ref[...], 1, 0)

    @pl.when(block == 0)
    def _():
        row = lax.broadcasted_iota(jnp.int32, (rows, 128), 0)
        lane = lax.broadcasted_iota(jnp.int32, (rows, 128), 1)
        in_panel = (lane < TILE_COLS // 2) | ((lane < TILE_COLS) & (row >= half))
        out_ref[:, 0:128] = jnp.where(in_panel, panel_ref[...], out_ref[:, 0:128])


STEP = 512


PARAMS = pltpu.CompilerParams(vmem_limit_bytes=24 << 20)


def near(value):
    return pltpu.with_memory_space_constraint(value, pltpu.VMEM)


def finish(col, inverse, left, right, matrix):
    local_rows, local_cols = matrix.shape
    bf16 = jnp.bfloat16
    vmem = pl.BlockSpec(memory_space=pltpu.VMEM)
    step = STEP
    return pl.pallas_call(
        update_kernel,
        compiler_params=PARAMS,
        grid=(local_cols // step,),
        out_shape=jax.ShapeDtypeStruct((local_rows, local_cols), f32),
        in_specs=[
            pl.BlockSpec(memory_space=pltpu.SMEM),
            vmem,
            vmem,
            vmem,
            pl.BlockSpec((local_rows, step), lambda g: (0, g)),
        ],
        out_specs=pl.BlockSpec((local_rows, step), lambda g: (0, g)),
        scratch_shapes=[pltpu.VMEM((3 * WIDTH, step), bf16)] * 2
        + [
            pltpu.VMEM((local_rows, 3 * WIDTH), bf16),
            pltpu.VMEM((local_rows, 128), f32),
            pltpu.VMEM((WIDTH, local_rows), f32),
            pltpu.VMEM((local_rows, 3 * WIDTH), bf16),
        ],
    )(col, inverse, left, right, matrix)


def per_device(matrix):
    local_rows, local_cols = matrix.shape
    packed = pl.pallas_call(
        pack_kernel,
        grid=(1,),
        in_specs=[pl.BlockSpec((16, 128), lambda g: (0, 0))],
        out_specs=pl.BlockSpec((N_ROW, 4, 128), lambda g: (0, 0, 0)),
        out_shape=jax.ShapeDtypeStruct((N_ROW, 4, 128), f32),
    )(matrix)
    packed = lax.all_to_all(packed, "row", 0, 0)
    folded = (N_ROW, TILE_ROWS * local_cols // 128, 128)
    top = pl.pallas_call(
        spread_kernel,
        grid=(1,),
        in_specs=[pl.BlockSpec((16, local_cols), lambda g: (0, 0))],
        out_specs=pl.BlockSpec(folded, lambda g: (0, 0, 0)),
        out_shape=jax.ShapeDtypeStruct(folded, f32),
    )(matrix)
    tall = (TILE_COLS * local_rows // 128, 128)
    turned = pl.pallas_call(
        turn_kernel,
        grid=(1,),
        in_specs=[pl.BlockSpec((local_rows, 128), lambda g: (0, 0))],
        out_specs=pl.BlockSpec(tall, lambda g: (0, 0)),
        out_shape=jax.ShapeDtypeStruct(tall, f32),
    )(matrix)
    packed, top, turned = lax.optimization_barrier((packed, top, turned))
    right = lax.all_to_all(top, "row", 0, 0).reshape(-1, 128)
    right = near(right)

    tile = pl.pallas_call(
        unpack_kernel,
        compiler_params=PARAMS,
        in_specs=[pl.BlockSpec(memory_space=pltpu.VMEM)],
        out_shape=jax.ShapeDtypeStruct((2 * TILE_COLS, 128), f32),
    )(near(packed.reshape(N_ROW * 4, 128)))
    corner = lax.all_gather(tile, "col", axis=0, tiled=True)
    corner, turned = lax.optimization_barrier((corner, turned))
    left = lax.all_gather(turned, "col", axis=0, tiled=True)
    inverse = pl.pallas_call(
        factor_kernel,
        compiler_params=PARAMS,
        in_specs=[pl.BlockSpec(memory_space=pltpu.VMEM)],
        out_shape=jax.ShapeDtypeStruct((WIDTH, 3 * WIDTH), jnp.bfloat16),
        scratch_shapes=[pltpu.VMEM((3, 3, 128, 128), f32)],
    )(near(corner))
    col = lax.axis_index("col").reshape(1).astype(jnp.int32)
    inverse = near(inverse)
    return finish(col, inverse, left, right, matrix)


def solution(mesh):
    return jax.shard_map(
        per_device,
        mesh=mesh,
        in_specs=(P("row", "col"),),
        out_specs=P("row", "col"),
        check_vma=False,
    )
```

time: 106 us -> 89.1 us (0.84)
  Pallas kernels: 38.7 us -> 22.7 us
  blocking collectives: 46.1 us -> 44.5 us
    pallas_call x4 -> x3, Pallas kernels: 33.4 us -> 17.4 us  [the longest x1 9.28 us: per_device(): pl.pallas_call(factor_kernel, compiler_params=PARAMS, in_specs=[pl.BlockS...]
    all_gather x1, blocking collectives: 27.9 us -> 26.3 us  [per_device(): corner = lax.all_gather(tile, 'col', axis=0, tiled=True)]
  transfers between devices with their start and end apart: 2 -> 2, of which waited for: 1 -> 1; matrix products, arithmetic and copies ran while one was open for 0% -> 0% of each run, Pallas kernels for 26% -> 15%
where the time goes in v4:
time: 89.1 us; the launch traced here: 88.6 us
  blocking collectives  44.5 us (50%)
  Pallas kernels  22.7 us (25%)
  starting transfers between devices  15.2 us (17%)
  waiting for transfers between devices  4.98 us (6%)
  local copies, waits for them, and re-layouts  1.14 us (1%)
    all_gather x1, blocking collectives, per_device(): corner = lax.all_gather(tile, 'col', axis=0, tiled=True)  26.3 us
    all_gather x1, blocking collectives, per_device(): left = lax.all_gather(turned, 'col', axis=0, tiled=True)  18.2 us
    all_to_all x1, starting transfers between devices, per_device(): packed = lax.all_to_all(packed, 'row', 0, 0)  10.5 us
    pallas_call x1, Pallas kernels, per_device(): pl.pallas_call(factor_kernel, compiler_params=PARAMS, in_specs=[pl.BlockS...  9.28 us
    pallas_call x1, Pallas kernels, finish(): pl.pallas_call(update_kernel, compiler_params=PARAMS, grid=(local_cols //...  7.94 us
    all_to_all x1, waiting for transfers between devices, per_device(): packed = lax.all_to_all(packed, 'row', 0, 0)  4.98 us
    all_to_all x1, starting transfers between devices, per_device(): right = lax.all_to_all(top, 'row', 0, 0).reshape(-1, 128)  4.7 us
    pallas_call x1, Pallas kernels, per_device(): pl.pallas_call(spread_kernel, grid=(1,), in_specs=[pl.BlockSpec((16, loca...  2.16 us
  transfers between devices with their start and end apart: 2, of which 1 were waited for; matrix products, arithmetic and copies ran while one was open for 0% of the time, Pallas kernels for 15%

profile of v4, /device:TPU:1, one launch (start us, length us, event | category | flops | bytes accessed | tf_op | source)
XLA Modules:
  0.0 88.6 jit_solution(6917560177292711695)
XLA Ops:
  0.0 1.4 %shard_map.17 = f32[32,4,128]{2,1,0:T(4,128)} custom-call(f32[512,1024]{1,0:T(8,128)} %matrix_ref.1), custom_call_target="tpu_custom_call" | custom-call | tf_op jit(solution)/shard_map/pallas_call | solution.py:285
  1.4 10.5 %all-to-all-start = ((f32[32,4,128]{2,1,0:T(4,128)}), f32[32,4,128]{2,1,0:T(4,128)S(1)}, u32[]{:S(2)}, u32[]{:S(2)}) async-start(f32[32,4,128]{2,1,0:T(4,128)} %shard_map.17), calls=%async_computation | async-start | bytes 131072 | tf_op jit(solution)/shard_map/all_to_all | solution.py:292
  11.9 1.7 %shard_map.19 = f32[96,128]{1,0:T(8,128)} custom-call(f32[512,1024]{1,0:T(8,128)} %matrix_ref.1), custom_call_target="tpu_custom_call" | custom-call | tf_op jit(solution)/shard_map/pallas_call | solution.py:302
  13.6 2.2 %shard_map.18 = f32[32,96,128]{2,1,0:T(8,128)} custom-call(f32[512,1024]{1,0:T(8,128)} %matrix_ref.1), custom_call_target="tpu_custom_call" | custom-call | tf_op jit(solution)/shard_map/pallas_call | solution.py:294
  15.8 0.0 copy-start.2
  15.8 5.0 %all-to-all-done = f32[32,4,128]{2,1,0:T(4,128)S(1)} async-done(((f32[32,4,128]{2,1,0:T(4,128)}), f32[32,4,128]{2,1,0:T(4,128)S(1)}, u32[]{:S(2)}, u32[]{:S(2)}) %all-to-all-start) | async-done | bytes 65568 | tf_op jit(solution)/shard_map/all_to_all | solution.py:292
  20.7 4.7 %all-to-all-start.1 = ((f32[32,96,128]{2,1,0:T(8,128)}), f32[32,96,128]{2,1,0:T(8,128)}, u32[]{:S(2)}, u32[]{:S(2)}) async-start(f32[32,96,128]{2,1,0:T(8,128)} %shard_map.18), calls=%async_computation.1 | async-start | bytes 3145728 | tf_op jit(solution)/shard_map/all_to_all | solution.py:310
  25.5 0.0 copy-start
  25.5 0.2 shard_map.20
  25.7 26.3 %all_gather.6.corner_ref = f32[768,128]{1,0:T(8,128)S(1)} all-gather(f32[48,128]{1,0:T(8,128)S(1)} %shard_map.20), channel_id=1, replica_groups=mesh['row'=32,'col'=16] {'col'}, dimensions={0}, use_global_device_ids=true | all-gather | bytes 417792 | tf_op jit(solution)/shard_map/all_gather | solution.py:319
  52.0 9.3 %shard_map.21.inv_ref = bf16[384,1152]{1,0:T(8,128)(2,1)S(1)} custom-call(f32[768,128]{1,0:T(8,128)S(1)} %all_gather.6.corner_ref), custom_call_target="tpu_custom_call" | custom-call | tf_op jit(solution)/shard_map/pallas_call | solution.py:322
  61.3 0.0 copy-done.2
  61.3 18.2 %all_gather.7.left_ref = f32[1536,128]{1,0:T(8,128)} all-gather(f32[96,128]{1,0:T(8,128)S(1)} %copy-done.2), channel_id=1, replica_groups=mesh['row'=32,'col'=16] {'col'}, dimensions={0}, use_global_device_ids=true | all-gather | bytes 835584 | tf_op jit(solution)/shard_map/all_gather | solution.py:321
  79.5 0.0 all-to-all-done.1
  79.5 0.0 copy-done
  79.5 0.0 copy-start.1
  79.5 1.1 %copy-done.1 = f32[1536,128]{1,0:T(8,128)S(1)} copy-done((f32[1536,128]{1,0:T(8,128)S(1)}, f32[1536,128]{1,0:T(8,128)}, u32[]{:S(2)}) %copy-start.1) | copy-done | bytes 786456
  80.6 7.9 %shard_map.22 = f32[512,1024]{1,0:T(8,128)} custom-call(s32[1]{0:T(128)} %bitcast.col_ref, bf16[384,1152]{1,0:T(8,128)(2,1)S(1)} %shard_map.21.inv_ref, f32[1536,128]{1,0:T(8,128)S(1)} %copy-done.1, f32[3072,128]{1,0:T(8,128)} %bitcast.2.right_ref, f32[512,1024]{1,0:T(8,128)S(1)} %copy-done), custom_call_target="tpu_custom_call" | custom-call | tf_op jit(solution)/shard_map/pallas_call | solution.py:260
Async XLA Ops:
  1.4 19.3 %all-to-all-start = ((f32[32,4,128]{2,1,0:T(4,128)}), f32[32,4,128]{2,1,0:T(4,128)S(1)}, u32[]{:S(2)}, u32[]{:S(2)}) async-start(f32[32,4,128]{2,1,0:T(4,128)} %shard_map.17), calls=%async_computation | async-start | bytes 131072 | tf_op jit(solution)/shard_map/all_to_all | solution.py:292
  15.8 45.5 %copy-start.2 = (f32[96,128]{1,0:T(8,128)S(1)}, f32[96,128]{1,0:T(8,128)}, u32[]{:S(2)}) copy-start(f32[96,128]{1,0:T(8,128)} %shard_map.19) | copy-start | bytes 147460
  20.7 58.8 %all-to-all-start.1 = ((f32[32,96,128]{2,1,0:T(8,128)}), f32[32,96,128]{2,1,0:T(8,128)}, u32[]{:S(2)}, u32[]{:S(2)}) async-start(f32[32,96,128]{2,1,0:T(8,128)} %shard_map.18), calls=%async_computation.1 | async-start | bytes 3145728 | tf_op jit(solution)/shard_map/all_to_all | solution.py:310
  25.5 54.1 %copy-start = (f32[512,1024]{1,0:T(8,128)S(1)}, f32[512,1024]{1,0:T(8,128)}, u32[]{:S(2)}) copy-start(f32[512,1024]{1,0:T(8,128)} %matrix_ref.1) | copy-start | bytes 6291460
  79.5 1.1 %copy-start.1 = (f32[1536,128]{1,0:T(8,128)S(1)}, f32[1536,128]{1,0:T(8,128)}, u32[]{:S(2)}) copy-start(f32[1536,128]{1,0:T(8,128)} %all_gather.7.left_ref) | copy-start | bytes 2359300

commit v5 on v4

--- a/solution.py
+++ b/solution.py
@@ -11,6 +11,7 @@
 N_COL = 16
 TILE_ROWS = WIDTH // N_ROW
 TILE_COLS = WIDTH // N_COL
+EARLY = 2
 f32 = jnp.float32
 
 
@@ -120,23 +121,20 @@
             ref[rows, WIDTH * n + lanes.start : WIDTH * n + lanes.stop] = parts[n]
 
 
+def chunk(ref, b):
+    return ref[:TILE_ROWS, 128 * b : 128 * b + 128]
+
+
 def pack_kernel(head_ref, out_ref):
-    lane = lax.broadcasted_iota(jnp.int32, (1, 128), 1)
-    for a in range(4):
-        total = jnp.zeros((1, 128), f32)
-        for b in range(4):
-            i = 4 * a + b
-            if i < TILE_ROWS:
-                row = jnp.where(lane < TILE_COLS, head_ref[i : i + 1, :], 0.0)
-                total = total + (pltpu.roll(row, 32 * b, 1) if b else row)
-        out_ref[:, a, :] = jnp.broadcast_to(total, (N_ROW, 128))
+    top = jnp.concatenate([chunk(head_ref, b) for b in range(EARLY)], axis=0)
+    for r in range(N_ROW):
+        out_ref[r] = top
 
 
 def unpack_kernel(tile_ref, out_ref):
     for a in range(3):
-        part = tile_ref[pl.ds(a, N_ROW, stride=4), :]
         stack = jnp.concatenate(
-            [part] + [pltpu.roll(part, 128 - 32 * b, 1) for b in range(1, 4)], axis=0
+            [tile_ref[pl.ds(4 * a + b, N_ROW, stride=EARLY * TILE_ROWS), :] for b in range(4)], axis=0
         )
         count = 8 * (a + 1)
         out_ref[4 * a * (a + 1) : 4 * a * (a + 1) + count, :] = jnp.transpose(stack)[:count]
@@ -167,19 +165,14 @@
                 s[a, b] = -value if b == p else s[a, b] - value
 
 
-def spread_kernel(head_ref, out_ref):
+def spread_kernel(head_ref, side_ref, out_ref, turned_ref):
     chunks = out_ref.shape[1] // TILE_ROWS
-    top = jnp.concatenate(
-        [head_ref[:TILE_ROWS, 128 * b : 128 * b + 128] for b in range(chunks)], axis=0
-    )
+    top = jnp.concatenate([chunk(head_ref, EARLY + b) for b in range(chunks)], axis=0)
     for r in range(N_ROW):
         out_ref[r] = top
-
-
-def turn_kernel(side_ref, out_ref):
     for b in range(side_ref.shape[0] // 128):
         part = jnp.transpose(side_ref[128 * b : 128 * b + 128, :])
-        out_ref[TILE_COLS * b : TILE_COLS * b + TILE_COLS, :] = part[:TILE_COLS]
+        turned_ref[TILE_COLS * b : TILE_COLS * b + TILE_COLS, :] = part[:TILE_COLS]
 
 
 def left_product(col_ref, inv_ref, left_ref, q_ref, panel_ref, s_ref, t_ref):
@@ -208,7 +201,7 @@
 
 
 def update_kernel(
-    col_ref, inv_ref, left_ref, right_ref, matrix_ref, out_ref, r_ref, u_ref, q_ref, panel_ref, s_ref, t_ref
+    col_ref, inv_ref, left_ref, early_ref, right_ref, matrix_ref, out_ref, r_ref, u_ref, q_ref, panel_ref, s_ref, t_ref
 ):
     rows = matrix_ref.shape[0]
     half = TILE_ROWS // 2
@@ -219,17 +212,29 @@
         left_product(col_ref, inv_ref, left_ref, q_ref, panel_ref, s_ref, t_ref)
 
     chunks = r_ref.shape[1] // 128
-    stride = right_ref.shape[0] // N_ROW
-    for b in range(chunks):
+
+    def fetch(ref, b, number):
         for i in range(TILE_ROWS):
-            first = (block * chunks + b) * TILE_ROWS + i
             put(
                 r_ref,
                 slice(N_ROW * i, N_ROW * i + N_ROW),
                 slice(128 * b, 128 * b + 128),
-                right_ref[pl.ds(first, N_ROW, stride=stride), :],
+                ref[pl.ds(number * TILE_ROWS + i, N_ROW, stride=ref.shape[0] // N_ROW), :],
                 True,
             )
+
+    for b in range(chunks):
+        if b < EARLY:
+
+            @pl.when(block == 0)
+            def _():
+                fetch(early_ref, b, b)
+
+            @pl.when(block != 0)
+            def _():
+                fetch(right_ref, b, block * chunks + b - EARLY)
+        else:
+            fetch(right_ref, b, block * chunks + b - EARLY)
     value = narrow_dot(inv_ref[...], r_ref[...], 1, 0)
     put(u_ref, slice(0, WIDTH), slice(0, 128 * chunks), value, True)
     out_ref[...] = matrix_ref[...] - narrow_dot(q_ref[...], u_ref[...], 1, 0)
@@ -252,18 +257,18 @@
     return pltpu.with_memory_space_constraint(value, pltpu.VMEM)
 
 
-def finish(col, inverse, left, right, matrix):
+def finish(col, inverse, left, early, right, matrix):
     local_rows, local_cols = matrix.shape
     bf16 = jnp.bfloat16
     vmem = pl.BlockSpec(memory_space=pltpu.VMEM)
     step = STEP
     return pl.pallas_call(
         update_kernel,
-        compiler_params=PARAMS,
         grid=(local_cols // step,),
         out_shape=jax.ShapeDtypeStruct((local_rows, local_cols), f32),
         in_specs=[
             pl.BlockSpec(memory_space=pltpu.SMEM),
+            vmem,
             vmem,
             vmem,
             vmem,
@@ -277,58 +282,56 @@
             pltpu.VMEM((WIDTH, local_rows), f32),
             pltpu.VMEM((local_rows, 3 * WIDTH), bf16),
         ],
-    )(col, inverse, left, right, matrix)
+    )(col, inverse, left, early, right, matrix)
 
 
 def per_device(matrix):
     local_rows, local_cols = matrix.shape
-    packed = pl.pallas_call(
+    chunks = local_cols // 128
+    first = (N_ROW, TILE_ROWS * EARLY, 128)
+    early = pl.pallas_call(
         pack_kernel,
         grid=(1,),
-        in_specs=[pl.BlockSpec((16, 128), lambda g: (0, 0))],
-        out_specs=pl.BlockSpec((N_ROW, 4, 128), lambda g: (0, 0, 0)),
-        out_shape=jax.ShapeDtypeStruct((N_ROW, 4, 128), f32),
+        in_specs=[pl.BlockSpec((16, 128 * EARLY), lambda g: (0, 0))],
+        out_specs=pl.BlockSpec(first, lambda g: (0, 0, 0)),
+        out_shape=jax.ShapeDtypeStruct(first, f32),
     )(matrix)
-    packed = lax.all_to_all(packed, "row", 0, 0)
-    folded = (N_ROW, TILE_ROWS * local_cols // 128, 128)
-    top = pl.pallas_call(
+    early = lax.all_to_all(early, "row", 0, 0)
+    late = (N_ROW, TILE_ROWS * (chunks - EARLY), 128)
+    tall = (TILE_COLS * local_rows // 128, 128)
+    top, turned = pl.pallas_call(
         spread_kernel,
         grid=(1,),
-        in_specs=[pl.BlockSpec((16, local_cols), lambda g: (0, 0))],
-        out_specs=pl.BlockSpec(folded, lambda g: (0, 0, 0)),
-        out_shape=jax.ShapeDtypeStruct(folded, f32),
-    )(matrix)
-    tall = (TILE_COLS * local_rows // 128, 128)
-    turned = pl.pallas_call(
-        turn_kernel,
-        grid=(1,),
-        in_specs=[pl.BlockSpec((local_rows, 128), lambda g: (0, 0))],
-        out_specs=pl.BlockSpec(tall, lambda g: (0, 0)),
-        out_shape=jax.ShapeDtypeStruct(tall, f32),
-    )(matrix)
-    packed, top, turned = lax.optimization_barrier((packed, top, turned))
-    right = lax.all_to_all(top, "row", 0, 0).reshape(-1, 128)
-    right = near(right)
-
+        in_specs=[
+            pl.BlockSpec((16, local_cols), lambda g: (0, 0)),
+            pl.BlockSpec((local_rows, 128), lambda g: (0, 0)),
+        ],
+        out_specs=(
+            pl.BlockSpec(late, lambda g: (0, 0, 0)),
+            pl.BlockSpec(tall, lambda g: (0, 0)),
+        ),
+        out_shape=(jax.ShapeDtypeStruct(late, f32), jax.ShapeDtypeStruct(tall, f32)),
+    )(matrix, matrix)
+    left = lax.all_gather(turned, "col", axis=0, tiled=True)
+    early, top, left = lax.optimization_barrier((early, top, left))
+    right = near(lax.all_to_all(top, "row", 0, 0).reshape(-1, 128))
+    early = near(early.reshape(-1, 128))
     tile = pl.pallas_call(
         unpack_kernel,
         compiler_params=PARAMS,
         in_specs=[pl.BlockSpec(memory_space=pltpu.VMEM)],
         out_shape=jax.ShapeDtypeStruct((2 * TILE_COLS, 128), f32),
-    )(near(packed.reshape(N_ROW * 4, 128)))
-    corner = lax.all_gather(tile, "col", axis=0, tiled=True)
-    corner, turned = lax.optimization_barrier((corner, turned))
-    left = lax.all_gather(turned, "col", axis=0, tiled=True)
+    )(early)
+    corner = near(lax.all_gather(near(tile), "col", axis=0, tiled=True))
     inverse = pl.pallas_call(
         factor_kernel,
-        compiler_params=PARAMS,
         in_specs=[pl.BlockSpec(memory_space=pltpu.VMEM)],
         out_shape=jax.ShapeDtypeStruct((WIDTH, 3 * WIDTH), jnp.bfloat16),
         scratch_shapes=[pltpu.VMEM((3, 3, 128, 128), f32)],
-    )(near(corner))
+    )(corner)
+
     col = lax.axis_index("col").reshape(1).astype(jnp.int32)
-    inverse = near(inverse)
-    return finish(col, inverse, left, right, matrix)
+    return finish(col, inverse, left, early, right, matrix)
 
 
 def solution(mesh):

time: 89.1 us -> 89.8 us (level)
  starting transfers between devices: 15.2 us -> 20 us
  Pallas kernels: 22.7 us -> 21.4 us
  blocking collectives: 44.5 us -> 43.3 us
  local copies, waits for them, and re-layouts: 1.14 us -> 0 us
  waiting for transfers between devices: 4.98 us -> 4 us
    all_gather x1, blocking collectives: 26.3 us -> 15.6 us  [per_device(): corner = near(lax.all_gather(near(tile), 'col', axis=0, tiled=True))]
    all_gather x1, blocking collectives: 18.2 us -> 27.7 us  [per_device(): left = lax.all_gather(turned, 'col', axis=0, tiled=True)]
    all_to_all x2, starting transfers between devices: 15.2 us -> 20 us  [the longest x1 10.5 us: per_device(): early = lax.all_to_all(early, 'row', 0, 0)]
    pallas_call x4 -> x3, Pallas kernels: 20.3 us -> 19.2 us  [the longest x1 10.2 us: per_device(): pl.pallas_call(factor_kernel, in_specs=[pl.BlockSpec(memory_space=pltpu.V...]
    unnamed x6 -> x0, local copies, waits for them, and re-layouts: 1.14 us -> none
    all_to_all x2, waiting for transfers between devices: 4.98 us -> 4 us  [the longest x1 3.99 us: per_device(): right = near(lax.all_to_all(top, 'row', 0, 0).reshape(-1, 128))]
  transfers between devices with their start and end apart: 2 -> 2, of which waited for: 1 -> 1; matrix products, arithmetic and copies ran while one was open for 0% -> 0% of each run, Pallas kernels for 15% -> 14%
where the time goes in v5:
time: 89.8 us; the launch traced here: 88.7 us
  blocking collectives  43.3 us (48%)
  Pallas kernels  21.4 us (24%)
  starting transfers between devices  20 us (22%)
  waiting for transfers between devices  4 us (4%)
    all_gather x1, blocking collectives, per_device(): left = lax.all_gather(turned, 'col', axis=0, tiled=True)  27.7 us
    all_gather x1, blocking collectives, per_device(): corner = near(lax.all_gather(near(tile), 'col', axis=0, tiled=True))  15.6 us
    all_to_all x1, starting transfers between devices, per_device(): early = lax.all_to_all(early, 'row', 0, 0)  10.5 us
    pallas_call x1, Pallas kernels, per_device(): pl.pallas_call(factor_kernel, in_specs=[pl.BlockSpec(memory_space=pltpu.V...  10.2 us
    all_to_all x1, starting transfers between devices, per_device(): right = near(lax.all_to_all(top, 'row', 0, 0).reshape(-1, 128))  9.5 us
    pallas_call x1, Pallas kernels, finish(): pl.pallas_call(update_kernel, grid=(local_cols // step,), out_shape=jax.S...  7.45 us
    all_to_all x1, waiting for transfers between devices, per_device(): right = near(lax.all_to_all(top, 'row', 0, 0).reshape(-1, 128))  3.99 us
    pallas_call x1, Pallas kernels, per_device(): pl.pallas_call(spread_kernel, grid=(1,), in_specs=[pl.BlockSpec((16, loca...  2.14 us
  transfers between devices with their start and end apart: 2, of which 1 were waited for; matrix products, arithmetic and copies ran while one was open for 0% of the time, Pallas kernels for 14%

profile of v5, /device:TPU:1, one launch (start us, length us, event | category | flops | bytes accessed | tf_op | source)
XLA Modules:
  0.0 88.7 jit_solution(6618390648590452834)
XLA Ops:
  0.0 1.5 %shard_map.17 = f32[32,24,128]{2,1,0:T(8,128)} custom-call(f32[512,1024]{1,0:T(8,128)} %matrix_ref.1), custom_call_target="tpu_custom_call" | custom-call | tf_op jit(solution)/shard_map/pallas_call | solution.py:292
  1.5 10.5 %all-to-all-start = ((f32[32,24,128]{2,1,0:T(8,128)}), f32[32,24,128]{2,1,0:T(8,128)S(1)}, u32[]{:S(2)}, u32[]{:S(2)}) async-start(f32[32,24,128]{2,1,0:T(8,128)} %shard_map.17), calls=%async_computation | async-start | bytes 786432 | tf_op jit(solution)/shard_map/all_to_all | solution.py:299
  12.0 2.1 %shard_map.18 = (f32[32,72,128]{2,1,0:T(8,128)}, f32[96,128]{1,0:T(8,128)}) custom-call(f32[512,1024]{1,0:T(8,128)} %matrix_ref.1, f32[512,1024]{1,0:T(8,128)} %matrix_ref.1), custom_call_target="tpu_custom_call" | custom-call | tf_op jit(solution)/shard_map/pallas_call | solution.py:302
  14.1 27.7 %all_gather.6.left_ref = f32[1536,128]{1,0:T(8,128)} all-gather(f32[96,128]{1,0:T(8,128)} %get-tuple-element.11), channel_id=1, replica_groups=mesh['row'=32,'col'=16] {'col'}, dimensions={0}, use_global_device_ids=true | all-gather | bytes 835584 | tf_op jit(solution)/shard_map/all_gather | solution.py:315
  41.9 0.0 all-to-all-done
  41.9 9.5 %all-to-all-start.1 = ((f32[32,72,128]{2,1,0:T(8,128)}), f32[32,72,128]{2,1,0:T(8,128)S(1)}, u32[]{:S(2)}, u32[]{:S(2)}) async-start(f32[32,72,128]{2,1,0:T(8,128)} %get-tuple-element.14), calls=%async_computation.1 | async-start | bytes 2359296 | tf_op jit(solution)/shard_map/all_to_all | solution.py:317
  51.4 0.1 shard_map.19
  51.5 15.6 %all_gather.7.corner_ref = f32[768,128]{1,0:T(8,128)S(1)} all-gather(f32[48,128]{1,0:T(8,128)S(1)} %shard_map.19), channel_id=1, replica_groups=mesh['row'=32,'col'=16] {'col'}, dimensions={0}, use_global_device_ids=true | all-gather | bytes 417792 | tf_op jit(solution)/shard_map/all_gather | solution.py:325
  67.0 10.2 %shard_map.20.inv_ref = bf16[384,1152]{1,0:T(8,128)(2,1)} custom-call(f32[768,128]{1,0:T(8,128)S(1)} %all_gather.7.corner_ref), custom_call_target="tpu_custom_call" | custom-call | tf_op jit(solution)/shard_map/pallas_call | solution.py:326
  77.2 4.0 %all-to-all-done.1 = f32[32,72,128]{2,1,0:T(8,128)S(1)} async-done(((f32[32,72,128]{2,1,0:T(8,128)}), f32[32,72,128]{2,1,0:T(8,128)S(1)}, u32[]{:S(2)}, u32[]{:S(2)}) %all-to-all-start.1) | async-done | bytes 1179680 | tf_op jit(solution)/shard_map/all_to_all | solution.py:317
  81.2 7.4 %shard_map.21 = f32[512,1024]{1,0:T(8,128)} custom-call(s32[1]{0:T(128)} %bitcast.col_ref, bf16[384,1152]{1,0:T(8,128)(2,1)} %shard_map.20.inv_ref, f32[1536,128]{1,0:T(8,128)} %all_gather.6.left_ref, f32[768,128]{1,0:T(8,128)S(1)} %bitcast.5, f32[2304,128]{1,0:T(8,128)S(1)} %bitcast.3, f32[512,1024]{1,0:T(8,128)} %matrix_ref.1), custom_call_target="tpu_custom_call" | custom-call | tf_op jit(solution)/shard_map/pallas_call | solution.py:265
Async XLA Ops:
  1.5 40.4 %all-to-all-start = ((f32[32,24,128]{2,1,0:T(8,128)}), f32[32,24,128]{2,1,0:T(8,128)S(1)}, u32[]{:S(2)}, u32[]{:S(2)}) async-start(f32[32,24,128]{2,1,0:T(8,128)} %shard_map.17), calls=%async_computation | async-start | bytes 786432 | tf_op jit(solution)/shard_map/all_to_all | solution.py:299
  41.9 39.4 %all-to-all-start.1 = ((f32[32,72,128]{2,1,0:T(8,128)}), f32[32,72,128]{2,1,0:T(8,128)S(1)}, u32[]{:S(2)}, u32[]{:S(2)}) async-start(f32[32,72,128]{2,1,0:T(8,128)} %get-tuple-element.14), calls=%async_computation.1 | async-start | bytes 2359296 | tf_op jit(solution)/shard_map/all_to_all | solution.py:317

commit v6 on v5

--- a/solution.py
+++ b/solution.py
@@ -11,7 +11,7 @@
 N_COL = 16
 TILE_ROWS = WIDTH // N_ROW
 TILE_COLS = WIDTH // N_COL
-EARLY = 2
+EARLY = 4
 f32 = jnp.float32
 
 

time: 89.8 us -> 85.6 us (0.953)
  waiting for transfers between devices: 4 us -> 0.01 us
    all_to_all x1, waiting for transfers between devices: 3.99 us -> 0.01 us  [per_device(): right = near(lax.all_to_all(top, 'row', 0, 0).reshape(-1, 128))]
  transfers between devices with their start and end apart: 2 -> 2, of which waited for: 1 -> 0; matrix products, arithmetic and copies ran while one was open for 0% -> 0% of each run, Pallas kernels for 14% -> 15%
where the time goes in v6:
time: 85.6 us; the launch traced here: 85.2 us
  blocking collectives  43.3 us (51%)
  Pallas kernels  21.9 us (26%)
  starting transfers between devices  20 us (23%)
    all_gather x1, blocking collectives, per_device(): left = lax.all_gather(turned, 'col', axis=0, tiled=True)  27.7 us
    all_gather x1, blocking collectives, per_device(): corner = near(lax.all_gather(near(tile), 'col', axis=0, tiled=True))  15.5 us
    all_to_all x1, starting transfers between devices, per_device(): early = lax.all_to_all(early, 'row', 0, 0)  10.5 us
    pallas_call x1, Pallas kernels, per_device(): pl.pallas_call(factor_kernel, in_specs=[pl.BlockSpec(memory_space=pltpu.V...  10.2 us
    all_to_all x1, starting transfers between devices, per_device(): right = near(lax.all_to_all(top, 'row', 0, 0).reshape(-1, 128))  9.49 us
    pallas_call x1, Pallas kernels, finish(): pl.pallas_call(update_kernel, grid=(local_cols // step,), out_shape=jax.S...  7.84 us
    pallas_call x1, Pallas kernels, per_device(): pl.pallas_call(spread_kernel, grid=(1,), in_specs=[pl.BlockSpec((16, loca...  2.03 us
  transfers between devices with their start and end apart: 2, of which 0 were waited for; matrix products, arithmetic and copies ran while one was open for 0% of the time, Pallas kernels for 15%

profile of v6, /device:TPU:1, one launch (start us, length us, event | category | flops | bytes accessed | tf_op | source)
XLA Modules:
  0.0 85.2 jit_solution(7040607171395500630)
XLA Ops:
  0.0 1.7 %shard_map.17 = f32[32,48,128]{2,1,0:T(8,128)} custom-call(f32[512,1024]{1,0:T(8,128)} %matrix_ref.1), custom_call_target="tpu_custom_call" | custom-call | tf_op jit(solution)/shard_map/pallas_call | solution.py:292
  1.7 10.5 %all-to-all-start = ((f32[32,48,128]{2,1,0:T(8,128)}), f32[32,48,128]{2,1,0:T(8,128)S(1)}, u32[]{:S(2)}, u32[]{:S(2)}) async-start(f32[32,48,128]{2,1,0:T(8,128)} %shard_map.17), calls=%async_computation | async-start | bytes 1572864 | tf_op jit(solution)/shard_map/all_to_all | solution.py:299
  12.2 2.0 %shard_map.18 = (f32[32,48,128]{2,1,0:T(8,128)}, f32[96,128]{1,0:T(8,128)}) custom-call(f32[512,1024]{1,0:T(8,128)} %matrix_ref.1, f32[512,1024]{1,0:T(8,128)} %matrix_ref.1), custom_call_target="tpu_custom_call" | custom-call | tf_op jit(solution)/shard_map/pallas_call | solution.py:302
  14.2 27.7 %all_gather.6.left_ref = f32[1536,128]{1,0:T(8,128)} all-gather(f32[96,128]{1,0:T(8,128)} %get-tuple-element.11), channel_id=1, replica_groups=mesh['row'=32,'col'=16] {'col'}, dimensions={0}, use_global_device_ids=true | all-gather | bytes 835584 | tf_op jit(solution)/shard_map/all_gather | solution.py:315
  41.9 0.0 all-to-all-done
  42.0 9.5 %all-to-all-start.1 = ((f32[32,48,128]{2,1,0:T(8,128)}), f32[32,48,128]{2,1,0:T(8,128)S(1)}, u32[]{:S(2)}, u32[]{:S(2)}) async-start(f32[32,48,128]{2,1,0:T(8,128)} %get-tuple-element.14), calls=%async_computation.1 | async-start | bytes 1572864 | tf_op jit(solution)/shard_map/all_to_all | solution.py:317
  51.5 0.1 shard_map.19
  51.6 15.5 %all_gather.7.corner_ref = f32[768,128]{1,0:T(8,128)S(1)} all-gather(f32[48,128]{1,0:T(8,128)S(1)} %shard_map.19), channel_id=1, replica_groups=mesh['row'=32,'col'=16] {'col'}, dimensions={0}, use_global_device_ids=true | all-gather | bytes 417792 | tf_op jit(solution)/shard_map/all_gather | solution.py:325
  67.1 10.2 %shard_map.20.inv_ref = bf16[384,1152]{1,0:T(8,128)(2,1)} custom-call(f32[768,128]{1,0:T(8,128)S(1)} %all_gather.7.corner_ref), custom_call_target="tpu_custom_call" | custom-call | tf_op jit(solution)/shard_map/pallas_call | solution.py:326
  77.3 0.0 all-to-all-done.1
  77.3 7.8 %shard_map.21 = f32[512,1024]{1,0:T(8,128)} custom-call(s32[1]{0:T(128)} %bitcast.col_ref, bf16[384,1152]{1,0:T(8,128)(2,1)} %shard_map.20.inv_ref, f32[1536,128]{1,0:T(8,128)} %all_gather.6.left_ref, f32[1536,128]{1,0:T(8,128)S(1)} %bitcast.4, f32[1536,128]{1,0:T(8,128)S(1)} %bitcast.5, f32[512,1024]{1,0:T(8,128)} %matrix_ref.1), custom_call_target="tpu_custom_call" | custom-call | tf_op jit(solution)/shard_map/pallas_call | solution.py:265
Async XLA Ops:
  1.7 40.3 %all-to-all-start = ((f32[32,48,128]{2,1,0:T(8,128)}), f32[32,48,128]{2,1,0:T(8,128)S(1)}, u32[]{:S(2)}, u32[]{:S(2)}) async-start(f32[32,48,128]{2,1,0:T(8,128)} %shard_map.17), calls=%async_computation | async-start | bytes 1572864 | tf_op jit(solution)/shard_map/all_to_all | solution.py:299
  42.0 35.4 %all-to-all-start.1 = ((f32[32,48,128]{2,1,0:T(8,128)}), f32[32,48,128]{2,1,0:T(8,128)S(1)}, u32[]{:S(2)}, u32[]{:S(2)}) async-start(f32[32,48,128]{2,1,0:T(8,128)} %get-tuple-element.14), calls=%async_computation.1 | async-start | bytes 1572864 | tf_op jit(solution)/shard_map/all_to_all | solution.py:317
